TPU v7x, 32 devices: a whole 2x2x4 slice. The times are simulated.
32 devices in a mesh: groups: 2 (over x), seq: 16 (over z, y, core).
Axes of the slice: x: 2, y: 2, z: 4, core: 2. Of those that a mesh axis runs over, the one named last changes fastest.
Arguments:
- hidden: bfloat16 [4096, 8192], P(('groups', 'seq')), parts along dimension 0, may hold values from -6 to 6
- q_base: bfloat16 [4096, 8192], P(('groups', 'seq')), parts along dimension 0, may hold values from -8 to 8
- base_key_weight: bfloat16 [4096, 1024], P(('groups', 'seq')), parts along dimension 0, may hold values from -8 to 8
- base_value_weight: bfloat16 [4096, 1024], P(('groups', 'seq')), parts along dimension 0, may hold values from -6 to 6
- shrink_a: bfloat16 [32, 8192, 192], P('groups', 'seq'), parts along dimension 0, may hold values from -0.0625 to 0.0625
- expand_q: bfloat16 [32, 64, 8192], P('groups', None, 'seq'), parts along dimension 0, may hold values from -0.375 to 0.375
- key_value_up_weight: bfloat16 [32, 64, 2048], P('groups'), parts along dimension 0, may hold values from -0.375 to 0.375
- block_request: int32 [64], P('groups'), parts along dimension 0, may hold values from 0 to 7, never falling along the last dimension, each value on 1 to 16 neighbouring positions
- request_adapter: int32 [16], P('groups'), parts along dimension 0, may hold values from 0 to 15
Outputs:
- attended: bfloat16 [4096, 8192], P(('groups', 'seq')), parts along dimension 0
There are 2 independent parts, one for each index of `groups`. A program takes and returns all parts, laid end to end along the dimension named above; each array names one. Nothing has to cross between parts.
Inputs may be any that keep to these rules, and one draw needn't show every extreme that they name: `block_request`: each request holds 1 to 16 consecutive blocks, request numbers never fall along the blocks, and some request holds exactly 16 blocks.
All inputs are finite; a program needn't handle non-finite values.
Results may differ from a plain program's by a relative error of at most 0.012.
The roundings to bfloat16 on the way count: a program that leaves them out, or rounds other values in their place, can miss the bound.
Values may be sent and summed in bfloat16 or wider, within the bound.
No kernel may reach another device: no remote copies, remote signals or barrier semaphores. Data moves between devices by JAX's collectives and lax.ppermute only.
A program may use at most 128 MiB of HBM per device.

v0:
```python
import math

import jax
import jax.numpy as jnp
from jax import lax
from jax.sharding import PartitionSpec as P

QUERY_HEADS = 64
KEY_VALUE_HEADS = 8
HEAD_SIZE = 128
ADAPTER_RANK = 64
QBLK = 512


def body(
    hidden,
    q_base,
    base_key_weight,
    base_value_weight,
    shrink_a,
    expand_q,
    key_value_up_weight,
    block_request,
    request_adapter,
):
    token_per_device = hidden.shape[0]
    device_list = lax.axis_size("seq")
    my_index = lax.axis_index("seq")
    token_total = token_per_device * device_list
    block_count = block_request.shape[0]
    block_len = token_total // block_count
    most_blocks = min(32, block_count // 2)
    key_window = QBLK + most_blocks * block_len
    heads_dev = QUERY_HEADS // device_list
    device_groups = device_list // KEY_VALUE_HEADS
    key_value_head = my_index // device_groups
    request_count = request_adapter.shape[0]
    adapter_number = key_value_up_weight.shape[0]
    slice_width = shrink_a.shape[1]
    picked = block_request[:, None] == jnp.arange(request_count, dtype=jnp.int32)[None, :]
    adapter_of = jnp.sum(jnp.where(picked, request_adapter[None, :], 0), axis=1)
    feature_rows = lax.all_to_all(hidden, "seq", split_axis=1, concat_axis=0, tiled=True)
    partial_value = jnp.einsum(
        "btf,bfr->btr",
        feature_rows.reshape(block_count, block_len, slice_width),
        shrink_a[adapter_of],
        preferred_element_type=jnp.float32,
    ).reshape(token_total, 3 * ADAPTER_RANK)
    shrunk = lax.psum(partial_value, "seq").astype(jnp.bfloat16)
    key_replicas = jnp.repeat(
        base_key_weight.reshape(token_per_device, KEY_VALUE_HEADS, HEAD_SIZE), device_groups, axis=1
    ).reshape(token_per_device, device_list * HEAD_SIZE)
    value_replicas = jnp.repeat(
        base_value_weight.reshape(token_per_device, KEY_VALUE_HEADS, HEAD_SIZE),
        device_groups,
        axis=1,
    ).reshape(token_per_device, device_list * HEAD_SIZE)
    q_heads, k_one, v_one = (
        lax.all_to_all(q_base, "seq", split_axis=1, concat_axis=0, tiled=True),
        lax.all_to_all(key_replicas, "seq", split_axis=1, concat_axis=0, tiled=True),
        lax.all_to_all(value_replicas, "seq", split_axis=1, concat_axis=0, tiled=True),
    )
    low_blocks = shrunk.reshape(block_count, block_len, 3, ADAPTER_RANK)
    q_delta = jnp.einsum(
        "btr,brc->btc",
        low_blocks[:, :, 0],
        expand_q[adapter_of],
        preferred_element_type=jnp.float32,
    ).reshape(token_total, heads_dev * HEAD_SIZE)
    query_rows = (
        (q_heads.astype(jnp.float32) + q_delta)
        .astype(jnp.bfloat16)
        .reshape(token_total, heads_dev, HEAD_SIZE)
    )
    kv_table = lax.dynamic_index_in_dim(
        key_value_up_weight.reshape(adapter_number, ADAPTER_RANK, 2, KEY_VALUE_HEADS, HEAD_SIZE),
        key_value_head,
        axis=3,
        keepdims=False,
    )
    kv_delta = jnp.einsum(
        "btcr,brcd->btcd",
        low_blocks[:, :, 1:],
        kv_table[adapter_of],
        preferred_element_type=jnp.float32,
    ).reshape(token_total, 2, HEAD_SIZE)
    key_rows = (k_one.astype(jnp.float32) + kv_delta[:, 0]).astype(jnp.bfloat16)
    value_rows = (v_one.astype(jnp.float32) + kv_delta[:, 1]).astype(jnp.bfloat16)
    request_of = jnp.repeat(block_request, block_len)
    score_scale = 1.0 / math.sqrt(HEAD_SIZE)

    def attend(block_index):
        q_start = block_index * QBLK
        k_start = jnp.clip(q_start + QBLK - key_window, 0, token_total - key_window)
        q_rows = lax.dynamic_slice_in_dim(query_rows, q_start, QBLK, 0)
        k_rows = lax.dynamic_slice_in_dim(key_rows, k_start, key_window, 0)
        v_rows = lax.dynamic_slice_in_dim(value_rows, k_start, key_window, 0)
        q_request = lax.dynamic_slice_in_dim(request_of, q_start, QBLK, 0)
        k_request = lax.dynamic_slice_in_dim(request_of, k_start, key_window, 0)
        q_pos = q_start + jnp.arange(QBLK, dtype=jnp.int32)
        k_pos = k_start + jnp.arange(key_window, dtype=jnp.int32)
        allowed = (k_pos[None, :] <= q_pos[:, None]) & (k_request[None, :] == q_request[:, None])
        scores = (
            jnp.einsum("qhd,kd->hqk", q_rows, k_rows, preferred_element_type=jnp.float32)
            * score_scale
        )
        scores = jnp.where(allowed[None], scores, -1e30)
        row_max = jnp.max(scores, axis=-1, keepdims=True)
        weights = jnp.exp(scores - row_max)
        probs = (weights / jnp.sum(weights, axis=-1, keepdims=True)).astype(jnp.bfloat16)
        result = jnp.einsum("hqk,kd->qhd", probs, v_rows, preferred_element_type=jnp.float32)
        return result.astype(jnp.bfloat16).reshape(QBLK, heads_dev * HEAD_SIZE)

    blocks_out = lax.map(attend, jnp.arange(token_total // QBLK, dtype=jnp.int32))
    head_rows = blocks_out.reshape(token_total, heads_dev * HEAD_SIZE)
    return lax.all_to_all(head_rows, "seq", split_axis=0, concat_axis=1, tiled=True)


def solution(mesh):
    return jax.shard_map(
        body,
        mesh=mesh,
        in_specs=(
            P(("groups", "seq"), None),
            P(("groups", "seq"), None),
            P(("groups", "seq"), None),
            P(("groups", "seq"), None),
            P("groups", "seq", None),
            P("groups", None, "seq"),
            P("groups", None, None),
            P("groups"),
            P("groups"),
        ),
        out_specs=P(("groups", "seq"), None),
        check_vma=False,
    )
```

profile of v0, /device:TPU:23, one launch (start us, length us, event | category | flops | bytes accessed | tf_op | source)
XLA Modules:
  0.0 370.1 jit_solution(3717521788086597597)
XLA Ops:
  0.0 1.1 copy_bitcast_fusion.3
  1.2 0.9 broadcast_in_dim.73
  2.0 6.4 %all-to-all-start = ((bf16[128,16,128]{2,0,1:T(8,128)(2,1)}), bf16[128,16,128]{2,0,1:T(8,128)(2,1)}, u32[]{:S(2)}, u32[]{:S(2)}) async-start(bf16[128,16,128]{2,0,1:T(8,128)(2,1)} %bitcast.117), calls=%async_computation | async-start | bytes 1048576 | tf_op jit(solution)/shard_map/all_to_all | solution.py:61
  8.5 3.1 copy.96
  11.6 8.8 %all-to-all-done = bf16[128,16,128]{2,0,1:T(8,128)(2,1)} async-done(((bf16[128,16,128]{2,0,1:T(8,128)(2,1)}), bf16[128,16,128]{2,0,1:T(8,128)(2,1)}, u32[]{:S(2)}, u32[]{:S(2)}) %all-to-all-start) | async-done | bytes 524320 | tf_op jit(solution)/shard_map/all_to_all | solution.py:61
  20.4 6.7 %all-to-all-start.1 = ((bf16[128,16,512]{2,0,1:T(8,128)(2,1)}), bf16[128,16,512]{2,0,1:T(8,128)(2,1)}, u32[]{:S(2)}, u32[]{:S(2)}) async-start(bf16[128,16,512]{2,0,1:T(8,128)(2,1)} %bitcast.109), calls=%async_computation.1 | async-start | bytes 4194304 | tf_op jit(solution)/shard_map/all_to_all | solution.py:42
  27.2 4.1 %copy.70 = bf16[128,8192]{0,1:T(8,128)(2,1)} copy(bf16[128,8192]{1,0:T(8,128)(2,1)} %param.12) | data formatting | bytes 4194304 | tf_op args[1]
  31.2 41.2 %all-to-all-done.1 = bf16[128,16,512]{2,0,1:T(8,128)(2,1)} async-done(((bf16[128,16,512]{2,0,1:T(8,128)(2,1)}), bf16[128,16,512]{2,0,1:T(8,128)(2,1)}, u32[]{:S(2)}, u32[]{:S(2)}) %all-to-all-start.1) | async-done | bytes 2097184 | tf_op jit(solution)/shard_map/all_to_all | solution.py:42
  72.5 7.0 %all-to-all-start.3 = ((bf16[128,16,512]{0,2,1:T(8,128)(2,1)}), bf16[128,16,512]{0,2,1:T(8,128)(2,1)}, u32[]{:S(2)}, u32[]{:S(2)}) async-start(bf16[128,16,512]{0,2,1:T(8,128)(2,1)} %bitcast.107), calls=%async_computation.3 | async-start | bytes 4194304 | tf_op jit(solution)/shard_map/all_to_all | solution.py:59
  79.5 5.6 %copy.89 = bf16[128,8,16,128]{3,2,1,0:T(8,128)(2,1)} copy(bf16[128,8,16,128]{3,1,2,0:T(8,128)(2,1)} %bitcast.114) | data formatting | bytes 8388608
  85.0 3.5 constant_dynamic-slice_fusion
  88.5 1.0 copy.97
  89.5 2.7 gather_fusion
  92.3 3.6 gather_fusion.1
  95.9 3.3 gather_fusion.2
  99.3 0.8 copy_bitcast_fusion.2
  100.0 5.5 %fusion.26 = f32[32,192,64]{1,2,0:T(8,128)S(1)} fusion(bf16[32,512,192]{1,2,0:T(8,128)(2,1)} %gather_fusion.1, bf16[32,64,512]{2,1,0:T(8,128)(2,1)} %bitcast.13), kind=kOutput, calls=%fused_computation.50 | convolution fusion | flops 402653184 | bytes 9961472 | tf_op jit(solution)/shard_map/btf,bfr->btr/dot_general | solution.py:43
  105.6 1.7 copy.66
  107.3 65.3 %all-reduce.1 = bf16[2048,192]{0,1:T(8,128)(2,1)S(1)} all-reduce(f32[2048,192]{0,1:T(8,128)} %copy.66), channel_id=1, replica_groups=mesh['groups'=2,'seq'=16] {'seq'}, use_global_device_ids=true, to_apply=%region_1.2 | all-reduce | flops 393216 | bytes 2359296 | tf_op jit(solution)/shard_map/psum | solution.py:49
  172.6 1.6 reshape.146
  174.3 1.1 copy-done.2
  175.4 0.7 convolution_bitcast_fusion
  176.1 0.2 copy.68
  176.4 0.8 slice-done
  177.1 0.6 copy.85
  177.8 4.2 %fusion.22 = f32[32,64,512]{2,1,0:T(8,128)} fusion(bf16[32,64,512]{2,1,0:T(8,128)(2,1)} %gather_fusion.2, bf16[32,64,1,64]{3,1,0,2:T(8,128)(2,1)S(1)} %copy.85), kind=kOutput, calls=%fused_computation.38 | convolution fusion | flops 134217728 | bytes 6553600 | tf_op jit(solution)/shard_map/btr,brc->btc/dot_general | solution.py:64
  182.0 5.3 %reshape.150 = f32[2048,4,128]{2,1,0:T(4,128)} reshape(f32[32,64,512]{2,1,0:T(8,128)} %fusion.22) | data formatting | bytes 8388608 | tf_op jit(solution)/shard_map/reshape | solution.py:69
  187.3 5.3 %copy.73 = f32[2048,4,128]{0,2,1:T(8,128)} copy(f32[2048,4,128]{2,1,0:T(4,128)} %reshape.150) | data formatting | bytes 8388608 | tf_op jit(solution)/shard_map/reshape | solution.py:69
  192.6 0.9 broadcast_in_dim.77
  193.5 13.4 %all-to-all-start.2 = ((bf16[128,16,128]{2,0,1:T(8,128)(2,1)}), bf16[128,16,128]{2,0,1:T(8,128)(2,1)S(1)}, u32[]{:S(2)}, u32[]{:S(2)}) async-start(bf16[128,16,128]{2,0,1:T(8,128)(2,1)} %bitcast.19), calls=%async_computation.2 | async-start | bytes 1048576 | tf_op jit(solution)/shard_map/all_to_all | solution.py:60
  206.9 2.0 convert_bitcast_fusion
  208.9 4.4 %copy.71 = f32[16,128,512]{1,0,2:T(8,128)} copy(f32[16,128,512]{1,2,0:T(8,128)S(1)} %convert_bitcast_fusion) | data formatting | bytes 8388608 | tf_op jit(solution)/shard_map/convert_element_type | solution.py:71
  213.3 4.9 %reshape.153 = f32[2048,4,128]{0,2,1:T(8,128)} reshape(f32[16,128,512]{1,0,2:T(8,128)} %copy.71) | data formatting | bytes 8388608 | tf_op jit(solution)/shard_map/convert_element_type | solution.py:71
  218.3 5.4 %add_convert_fusion = bf16[2048,4,128]{0,2,1:T(8,128)(2,1)} fusion(f32[2048,4,128]{0,2,1:T(8,128)} %reshape.153, f32[2048,4,128]{0,2,1:T(8,128)} %copy.73), kind=kLoop, calls=%fused_computation.28 | loop fusion | flops 2097152 | bytes 10485760 | tf_op jit(solution)/shard_map/convert_element_type | solution.py:72
  223.7 2.0 fusion.18
  225.7 84.3 %while.14 = (s32[]{:T(128)}, bf16[4,512,512]{2,1,0:T(8,128)(2,1)}, s32[4]{0:T(128)S(1)}, bf16[2048,128]{1,0:T(8,128)(2,1)}, s32[2048]{0:T(1024)S(1)}, /*index=5*...) while((s32[]{:T(128)}, bf16[4,512,512]{2,1,0:T(8,128)(2,1)}, ...), condition=%wide.region_5.6_spmd, body=%wide.region_2.5_spmd.sunk | while | flops 1638403584 | bytes 57991952 | solution.py:114
  225.7 0.7 dynamic_slice.80
  227.2 1.2 compare_and_fusion.2
  228.4 2.8 fusion.42
  231.2 8.9 %fusion.43 = (f32[4,512]{1,0:T(4,128)S(1)}, f32[4,512,1536]{1,2,0:T(8,128)}) fusion(f32[1536,512,4]{1,0,2:T(8,128)S(1)} %fusion.42, pred[512,1536]{0,1:T(8,128)(4,1)S(1)} %compare_and_fusion.2), kind=kOutput, calls=%fused_computation.49.clone.1 | output fusion | flops 18875904 | bytes 25960448 | tf_op jit(solution)/shard_map/while/body/eval_jaxpr/sub | solution.py:109
  240.1 5.6 %fusion.44 = bf16[128,4,512]{2,0,1:T(8,128)(2,1)S(1)} fusion(f32[4,512,1536]{1,2,0:T(8,128)} %get-tuple-element.245, f32[4,512]{1,0:T(4,128)S(1)} %get-tuple-element.246, bf16[2048,128]{1,0:T(8,128)(2,1)S(1)} %copy-done.5, s32[]{:T(128)S(6)} %min.11), kind=kOutput, calls=%fused_computation.13.clone.1 | convolution fusion | flops 811859968 | bytes 13508612 | tf_op jit(solution)/shard_map/while/body/eval_jaxpr/hqk,kd->qhd/dot_general | solution.py:111
  246.0 0.8 constant_dynamic-update-slice_fusion.2
  246.8 0.7 dynamic_slice.80
  248.3 1.2 compare_and_fusion.2
  249.5 2.8 fusion.42
  252.3 8.9 %fusion.43 = (f32[4,512]{1,0:T(4,128)S(1)}, f32[4,512,1536]{1,2,0:T(8,128)}) fusion(f32[1536,512,4]{1,0,2:T(8,128)S(1)} %fusion.42, pred[512,1536]{0,1:T(8,128)(4,1)S(1)} %compare_and_fusion.2), kind=kOutput, calls=%fused_computation.49.clone.1 | output fusion | flops 18875904 | bytes 25960448 | tf_op jit(solution)/shard_map/while/body/eval_jaxpr/sub | solution.py:109
  261.2 5.6 %fusion.44 = bf16[128,4,512]{2,0,1:T(8,128)(2,1)S(1)} fusion(f32[4,512,1536]{1,2,0:T(8,128)} %get-tuple-element.245, f32[4,512]{1,0:T(4,128)S(1)} %get-tuple-element.246, bf16[2048,128]{1,0:T(8,128)(2,1)S(1)} %copy-done.5, s32[]{:T(128)S(6)} %min.11), kind=kOutput, calls=%fused_computation.13.clone.1 | convolution fusion | flops 811859968 | bytes 13508612 | tf_op jit(solution)/shard_map/while/body/eval_jaxpr/hqk,kd->qhd/dot_general | solution.py:111
  267.1 0.8 constant_dynamic-update-slice_fusion.2
  267.9 0.7 dynamic_slice.80
  269.4 1.2 compare_and_fusion.2
  270.6 2.8 fusion.42
  273.4 8.9 %fusion.43 = (f32[4,512]{1,0:T(4,128)S(1)}, f32[4,512,1536]{1,2,0:T(8,128)}) fusion(f32[1536,512,4]{1,0,2:T(8,128)S(1)} %fusion.42, pred[512,1536]{0,1:T(8,128)(4,1)S(1)} %compare_and_fusion.2), kind=kOutput, calls=%fused_computation.49.clone.1 | output fusion | flops 18875904 | bytes 25960448 | tf_op jit(solution)/shard_map/while/body/eval_jaxpr/sub | solution.py:109
  282.3 5.6 %fusion.44 = bf16[128,4,512]{2,0,1:T(8,128)(2,1)S(1)} fusion(f32[4,512,1536]{1,2,0:T(8,128)} %get-tuple-element.245, f32[4,512]{1,0:T(4,128)S(1)} %get-tuple-element.246, bf16[2048,128]{1,0:T(8,128)(2,1)S(1)} %copy-done.5, s32[]{:T(128)S(6)} %min.11), kind=kOutput, calls=%fused_computation.13.clone.1 | convolution fusion | flops 811859968 | bytes 13508612 | tf_op jit(solution)/shard_map/while/body/eval_jaxpr/hqk,kd->qhd/dot_general | solution.py:111
  287.9 0.2 copy.99
  288.1 0.8 constant_dynamic-update-slice_fusion.2
  289.0 0.7 dynamic_slice.80
  290.5 1.2 compare_and_fusion.2
  291.7 2.8 fusion.42
  294.5 8.9 %fusion.43 = (f32[4,512]{1,0:T(4,128)S(1)}, f32[4,512,1536]{1,2,0:T(8,128)}) fusion(f32[1536,512,4]{1,0,2:T(8,128)S(1)} %fusion.42, pred[512,1536]{0,1:T(8,128)(4,1)S(1)} %compare_and_fusion.2), kind=kOutput, calls=%fused_computation.49.clone.1 | output fusion | flops 18875904 | bytes 25960448 | tf_op jit(solution)/shard_map/while/body/eval_jaxpr/sub | solution.py:109
  303.4 5.6 %fusion.44 = bf16[128,4,512]{2,0,1:T(8,128)(2,1)S(1)} fusion(f32[4,512,1536]{1,2,0:T(8,128)} %get-tuple-element.245, f32[4,512]{1,0:T(4,128)S(1)} %get-tuple-element.246, bf16[2048,128]{1,0:T(8,128)(2,1)S(1)} %copy-done.5, s32[]{:T(128)S(6)} %min.11), kind=kOutput, calls=%fused_computation.13.clone.1 | convolution fusion | flops 811859968 | bytes 13508612 | tf_op jit(solution)/shard_map/while/body/eval_jaxpr/hqk,kd->qhd/dot_general | solution.py:111
  309.2 0.8 constant_dynamic-update-slice_fusion.2
  310.1 51.9 %all_to_all.74 = bf16[16,128,512]{2,1,0:T(8,128)(2,1)} all-to-all(bf16[16,128,512]{2,1,0:T(8,128)(2,1)} %bitcast.116), channel_id=1, replica_groups=mesh['groups'=2,'seq'=16] {'seq'}, dimensions={0} | all-to-all | bytes 4194304 | tf_op jit(solution)/shard_map/all_to_all | solution.py:116
  361.9 4.0 %copy.77 = bf16[128,16,512]{0,2,1:T(8,128)(2,1)} copy(bf16[128,16,512]{2,0,1:T(8,128)(2,1)} %bitcast.110) | data formatting | bytes 4194304 | tf_op jit(solution)/shard_map/all_to_all | solution.py:116
  366.0 4.1 %copy.78 = bf16[128,8192]{1,0:T(8,128)(2,1)} copy(bf16[128,8192]{0,1:T(8,128)(2,1)} %bitcast.111) | data formatting | bytes 4194304 | tf_op jit(solution)/shard_map/all_to_all | solution.py:116
  (53 shorter events, 1.6 us)
Async XLA Ops:
  0.0 92.3 %copy-start = (bf16[16,512,192]{1,2,0:T(8,128)(2,1)S(1)}, bf16[16,512,192]{1,2,0:T(8,128)(2,1)}, u32[]{:S(2)}) copy-start(bf16[16,512,192]{1,2,0:T(8,128)(2,1)} %param.15) | copy-start | bytes 9437188
  2.0 18.4 %all-to-all-start = ((bf16[128,16,128]{2,0,1:T(8,128)(2,1)}), bf16[128,16,128]{2,0,1:T(8,128)(2,1)}, u32[]{:S(2)}, u32[]{:S(2)}) async-start(bf16[128,16,128]{2,0,1:T(8,128)(2,1)} %bitcast.117), calls=%async_computation | async-start | bytes 1048576 | tf_op jit(solution)/shard_map/all_to_all | solution.py:61
  20.4 52.1 %all-to-all-start.1 = ((bf16[128,16,512]{2,0,1:T(8,128)(2,1)}), bf16[128,16,512]{2,0,1:T(8,128)(2,1)}, u32[]{:S(2)}, u32[]{:S(2)}) async-start(bf16[128,16,512]{2,0,1:T(8,128)(2,1)} %bitcast.109), calls=%async_computation.1 | async-start | bytes 4194304 | tf_op jit(solution)/shard_map/all_to_all | solution.py:42
  72.5 120.1 %all-to-all-start.3 = ((bf16[128,16,512]{0,2,1:T(8,128)(2,1)}), bf16[128,16,512]{0,2,1:T(8,128)(2,1)}, u32[]{:S(2)}, u32[]{:S(2)}) async-start(bf16[128,16,512]{0,2,1:T(8,128)(2,1)} %bitcast.107), calls=%async_computation.3 | async-start | bytes 4194304 | tf_op jit(solution)/shard_map/all_to_all | solution.py:59
  85.0 4.4 %copy-start.7 = (s32[32]{0:T(128)S(1)}, s32[32]{0:T(128)}, u32[]{:S(2)}) copy-start(s32[32]{0:T(128)} %param.18) | copy-start | bytes 388
  85.0 4.4 %copy-start.8 = (s32[8]{0:T(128)S(1)}, s32[8]{0:T(128)}, u32[]{:S(2)}) copy-start(s32[8]{0:T(128)} %param.19) | copy-start | bytes 100
  95.9 3.4 copy-start.6
  172.6 2.8 copy-start.3
  174.2 1.2 copy-start.2
  176.1 1.0 slice-start
  187.3 5.4 %copy-start.4 = (bf16[128,8,128]{2,0,1:T(8,128)(2,1)S(1)}, bf16[128,8,128]{2,0,1:T(8,128)(2,1)}, u32[]{:S(2)}) copy-start(bf16[128,8,128]{2,0,1:T(8,128)(2,1)} %copy_bitcast_fusion.2) | copy-start | bytes 786436
  193.5 30.2 %all-to-all-start.2 = ((bf16[128,16,128]{2,0,1:T(8,128)(2,1)}), bf16[128,16,128]{2,0,1:T(8,128)(2,1)S(1)}, u32[]{:S(2)}, u32[]{:S(2)}) async-start(bf16[128,16,128]{2,0,1:T(8,128)(2,1)} %bitcast.19), calls=%async_computation.2 | async-start | bytes 1048576 | tf_op jit(solution)/shard_map/all_to_all | solution.py:60
  231.2 8.9 %copy-start.5 = (bf16[2048,128]{1,0:T(8,128)(2,1)S(1)}, bf16[2048,128]{1,0:T(8,128)(2,1)}, u32[]{:S(2)}) copy-start(bf16[2048,128]{1,0:T(8,128)(2,1)} %get-tuple-element.276) | copy-start | bytes 1572868 | tf_op jit(solution)/shard_map/while
  252.3 8.9 %copy-start.5 = (bf16[2048,128]{1,0:T(8,128)(2,1)S(1)}, bf16[2048,128]{1,0:T(8,128)(2,1)}, u32[]{:S(2)}) copy-start(bf16[2048,128]{1,0:T(8,128)(2,1)} %get-tuple-element.276) | copy-start | bytes 1572868 | tf_op jit(solution)/shard_map/while
  273.4 8.9 %copy-start.5 = (bf16[2048,128]{1,0:T(8,128)(2,1)S(1)}, bf16[2048,128]{1,0:T(8,128)(2,1)}, u32[]{:S(2)}) copy-start(bf16[2048,128]{1,0:T(8,128)(2,1)} %get-tuple-element.276) | copy-start | bytes 1572868 | tf_op jit(solution)/shard_map/while
  294.5 8.9 %copy-start.5 = (bf16[2048,128]{1,0:T(8,128)(2,1)S(1)}, bf16[2048,128]{1,0:T(8,128)(2,1)}, u32[]{:S(2)}) copy-start(bf16[2048,128]{1,0:T(8,128)(2,1)} %get-tuple-element.276) | copy-start | bytes 1572868 | tf_op jit(solution)/shard_map/while
  361.9 8.1 %copy-start.1 = (bf16[16,512,192]{1,2,0:T(8,128)(2,1)S(1)}, bf16[16,512,192]{1,2,0:T(8,128)(2,1)}, u32[]{:S(2)}) copy-start(bf16[16,512,192]{1,2,0:T(8,128)(2,1)} %param.15) | copy-start | bytes 9437188
where the time goes:
time: 375 us; the launch traced here: 370 us
  blocking collectives  117 us (31%)
  local copies, waits for them, and re-layouts  72.3 us (19%)
  waiting for transfers between devices  50.1 us (13%)
  other arithmetic  49.8 us (13%)
  matrix products  44.2 us (12%)
  starting transfers between devices  33.5 us (9%)
    psum x1, blocking collectives, body(): shrunk = lax.psum(partial_value, 'seq').astype(jnp.bfloat16)  65.3 us
    all_to_all x1, blocking collectives, body(): lax.all_to_all(head_rows, 'seq', split_axis=0, concat_axis=1, tiled=True)  51.9 us
    all_to_all x1, waiting for transfers between devices, body(): lax.all_to_all(hidden, 'seq', split_axis=1, concat_axis=0, tiled=True)  41.2 us
    sub x4, other arithmetic, attend(): weights = jnp.exp(scores - row_max)  35.6 us
    dot_general x4, matrix products, attend(): jnp.einsum('hqk,kd->qhd', probs, v_rows, preferred_element_type=jnp.float32)  22.5 us
    all_to_all x1, starting transfers between devices, body(): lax.all_to_all(key_replicas, 'seq', split_axis=1, concat_axis=0, tiled=True)  13.4 us
    unnamed x19, local copies, waits for them, and re-layouts  11.3 us
    dot_general x4, matrix products, attend(): jnp.einsum('qhd,kd->hqk', q_rows, k_rows, preferred_element_type=jnp.floa...  11.3 us
  transfers between devices with their start and end apart: 4, of which 2 were waited for; matrix products, arithmetic and copies ran while one was open for 19% of the time, Pallas kernels for 0%

commit v1 on v0

v1 whole, which is shorter than its diff:
```python
import functools
import math

import jax
import jax.numpy as jnp
from jax import lax
from jax.experimental import pallas as pl
from jax.experimental.pallas import tpu as pltpu
from jax.sharding import PartitionSpec as P

KEY_VALUE_HEADS = 8
HEAD_SIZE = 128
ADAPTER_RANK = 64
MOST_BLOCKS_CAP = 32
CORES = 2
PLANE = 4
KEY_CHUNK = 256
NT = (((1,), (1,)), ((), ()))
TN = (((0,), (0,)), ((), ()))


def split_kernel(hidden_ref, key_ref, value_ref, sent_ref, kv_ref):
    sent_ref[0] = hidden_ref[...]

    @pl.when(pl.program_id(0) == 0)
    def _():
        width = key_ref.shape[1]
        kv_ref[:, :width] = key_ref[...]
        kv_ref[:, width:] = value_ref[...]


def split(hidden, base_key, base_value, parts):
    tokens, width = hidden.shape
    span = width // parts
    kv_width = base_key.shape[1]
    return pl.pallas_call(
        split_kernel,
        out_shape=(
            jax.ShapeDtypeStruct((parts, tokens, span), hidden.dtype),
            jax.ShapeDtypeStruct((tokens, 2 * kv_width), hidden.dtype),
        ),
        grid=(parts,),
        in_specs=[
            pl.BlockSpec((tokens, span), lambda i: (0, i)),
            pl.BlockSpec((tokens, kv_width), lambda i: (0, 0)),
            pl.BlockSpec((tokens, kv_width), lambda i: (0, 0)),
        ],
        out_specs=(
            pl.BlockSpec((1, tokens, span), lambda i: (i, 0, 0)),
            pl.BlockSpec((tokens, 2 * kv_width), lambda i: (0, 0)),
        ),
        name="split",
    )(hidden, base_key, base_value)


def shrink_kernel(block_len, place_ref, request_ref, adapter_ref, rows_ref, own_ref, other_ref, out_ref):
    sources, tokens, features = rows_ref.shape
    per_device = tokens // block_len
    half = features // CORES
    core = lax.rem(place_ref[0], CORES)
    own_columns = pl.ds(pl.multiple_of(core * half, half), half)
    other_columns = pl.ds(pl.multiple_of((1 - core) * half, half), half)
    first = pl.program_id(0) * sources
    for source in range(sources):
        device = (first + source) * CORES + core
        for part in range(per_device):
            adapter = adapter_ref[request_ref[device * per_device + part]]
            span = pl.ds(part * block_len, block_len)
            total = lax.dot_general(
                own_ref[adapter], rows_ref[source, span, own_columns], NT, preferred_element_type=jnp.float32
            ) + lax.dot_general(
                other_ref[adapter], rows_ref[source, span, other_columns], NT, preferred_element_type=jnp.float32
            )
            out_ref[source, :, span] = total.astype(out_ref.dtype)


def shrink(rows, own, other, place, block_request, request_adapter, block_len):
    chips, tokens, features = rows.shape
    adapters, width, half = own.shape
    steps = min(2, chips)
    sources = chips // steps
    return pl.pallas_call(
        functools.partial(shrink_kernel, block_len),
        out_shape=jax.ShapeDtypeStruct((chips, width, tokens), jnp.bfloat16),
        grid_spec=pltpu.PrefetchScalarGridSpec(
            num_scalar_prefetch=3,
            grid=(steps,),
            in_specs=[
                pl.BlockSpec((sources, tokens, features), lambda i, me, br, ra: (i, 0, 0)),
                pl.BlockSpec((adapters, width, half), lambda i, me, br, ra: (0, 0, 0)),
                pl.BlockSpec((adapters, width, half), lambda i, me, br, ra: (0, 0, 0)),
            ],
            out_specs=pl.BlockSpec((sources, width, tokens), lambda i, me, br, ra: (i, 0, 0)),
        ),
        cost_estimate=pl.CostEstimate(
            flops=2 * chips * tokens * features * width,
            bytes_accessed=2 * (rows.size + own.size + other.size),
            transcendentals=0,
        ),
        name="shrink",
    )(place, block_request, request_adapter, rows, own, other)


def finish_kernel(block_len, planes, place_ref, request_ref, adapter_ref, low_ref, up_ref, *rest):
    pieces = planes * PLANE
    piece_refs = rest[:pieces]
    out_ref, base_ref, done_ref, in_sems, out_sems = rest[pieces:]
    tokens = piece_refs[0].shape[0]
    per_device = tokens // block_len
    rank = ADAPTER_RANK
    width = base_ref.shape[2] // 2
    me = place_ref[0]
    within = lax.rem(me, PLANE)
    for index in range(pieces):
        pltpu.make_async_copy(piece_refs[index], base_ref.at[index], in_sems.at[index]).start()
    for index in range(pieces):
        back, flip = index // PLANE, index % PLANE
        place = within ^ flip
        device = me - within - back * PLANE + place
        pltpu.make_async_copy(piece_refs[index], base_ref.at[index], in_sems.at[index]).wait()
        for part in range(per_device):
            adapter = adapter_ref[request_ref[jnp.maximum(device * per_device + part, 0)]]
            span = pl.ds(part * block_len, block_len)
            for which in range(2):
                columns = pl.ds(which * width, width)
                delta = lax.dot_general(
                    low_ref[index, pl.ds(which * rank, rank), span],
                    up_ref[adapter, :, columns],
                    TN,
                    preferred_element_type=jnp.float32,
                )
                done_ref[index, span, columns] = (
                    base_ref[index, span, columns].astype(jnp.float32) + delta
                ).astype(done_ref.dtype)
        slot = (planes - 1 - back) * PLANE + place
        pltpu.make_async_copy(
            done_ref.at[index], out_ref.at[pl.ds(pl.multiple_of(slot * tokens, tokens), tokens), :], out_sems.at[index]
        ).start()
    for index in range(pieces):
        pltpu.make_async_copy(done_ref.at[index], out_ref.at[pl.ds(0, tokens), :], out_sems.at[index]).wait()


def finish(pieces, lows, up_weight, place, block_request, request_adapter, block_len, planes):
    tokens, width = pieces[0].shape
    count = len(pieces)
    return pl.pallas_call(
        functools.partial(finish_kernel, block_len, planes),
        out_shape=jax.ShapeDtypeStruct((count * tokens, width), jnp.bfloat16),
        grid_spec=pltpu.PrefetchScalarGridSpec(
            num_scalar_prefetch=3,
            grid=(1,),
            in_specs=[
                pl.BlockSpec(lows.shape, lambda i, me, br, ra: (0, 0, 0)),
                pl.BlockSpec(up_weight.shape, lambda i, me, br, ra: (0, 0, 0)),
            ]
            + [pl.BlockSpec(memory_space=pl.ANY)] * count,
            out_specs=pl.BlockSpec(memory_space=pl.ANY),
            scratch_shapes=[
                pltpu.VMEM((count, tokens, width), jnp.bfloat16),
                pltpu.VMEM((count, tokens, width), jnp.bfloat16),
                pltpu.SemaphoreType.DMA((count,)),
                pltpu.SemaphoreType.DMA((count,)),
            ],
        ),
        cost_estimate=pl.CostEstimate(
            flops=2 * count * tokens * width * ADAPTER_RANK, bytes_accessed=4 * count * tokens * width, transcendentals=0
        ),
        name="finish",
    )(place, block_request, request_adapter, lows, up_weight, *pieces)


def attend_kernel(
    block_len, most_blocks, planes, place_ref, request_ref, q_ref, low_ref, up_ref, key_ref, value_ref,
    out_ref, query_ref, total_ref, top_ref, sum_ref,
):
    tokens = q_ref.shape[0]
    per_device = tokens // block_len
    me = place_ref[0]
    within = lax.rem(me, PLANE)
    group = q_ref.shape[1] // HEAD_SIZE
    rows = group * block_len
    sources = up_ref.shape[0]
    span = up_ref.shape[3]
    heads = span // HEAD_SIZE
    for part in range(per_device):
        own_rows = pl.ds(part * block_len, block_len)
        for source in range(sources):
            columns = pl.ds(source * span, span)
            delta = lax.dot_general(
                low_ref[:, own_rows], up_ref[source, part], TN, preferred_element_type=jnp.float32
            )
            query = (q_ref[own_rows, columns].astype(jnp.float32) + delta).astype(jnp.bfloat16)
            for at in range(heads):
                row = part * rows + (source * heads + at) * block_len
                query_ref[pl.ds(row, block_len), :] = query[:, at * HEAD_SIZE : (at + 1) * HEAD_SIZE]

    first_block = me * per_device
    request = request_ref[first_block]
    count = jnp.int32(1)
    for back in range(1, most_blocks):
        earlier = request_ref[jnp.maximum(first_block - back, 0)]
        count = count + ((first_block >= back) & (earlier == request)).astype(jnp.int32)
    window_first = ((planes - 1) * PLANE + within) * per_device
    end = (window_first + per_device) * block_len
    starts = [(window_first - count + 1) * block_len]
    for part in range(1, per_device):
        same = request_ref[first_block + part] == request_ref[first_block + part - 1]
        starts.append(jnp.where(same, starts[-1], (window_first + part) * block_len))
    all_same = request_ref[first_block + per_device - 1] == request
    chunks = lax.div(end - starts[0] + (KEY_CHUNK - 1), KEY_CHUNK)
    factor = math.log2(math.e) / math.sqrt(HEAD_SIZE)

    def chunk(step, parts, first, masked):
        stop = end - step * KEY_CHUNK
        start = stop - KEY_CHUNK
        if masked:
            start = jnp.maximum(start, 0)
        start = pl.multiple_of(start, block_len)
        keys = key_ref[pl.ds(start, KEY_CHUNK), :]
        values = value_ref[pl.ds(start, KEY_CHUNK), :]
        for part in parts:
            columns = pl.ds(part * rows, rows)
            scores = lax.dot_general(keys, query_ref[columns, :], NT, preferred_element_type=jnp.float32)
            if masked:
                key_at = start + lax.broadcasted_iota(jnp.int32, scores.shape, 0)
                allowed = (key_at >= starts[part]) & (key_at < stop)
                if first:
                    query_at = (window_first + part) * block_len + lax.rem(
                        lax.broadcasted_iota(jnp.int32, scores.shape, 1), block_len
                    )
                    allowed = allowed & (key_at <= query_at)
                scores = jnp.where(allowed, scores, -1e30)
            top = jnp.max(scores, axis=0, keepdims=True)
            if not first:
                top = jnp.maximum(top, top_ref[:, columns])
            weights = jnp.exp2((scores - top) * factor)
            sums = jnp.sum(weights, axis=0, keepdims=True)
            product = lax.dot_general(
                values, weights.astype(jnp.bfloat16), TN, preferred_element_type=jnp.float32
            )
            if not first:
                fade = jnp.exp2((top_ref[:, columns] - top) * factor)
                sums = sums + sum_ref[:, columns] * fade
                product = product + total_ref[:, columns] * fade
            top_ref[:, columns] = top
            sum_ref[:, columns] = sums
            total_ref[:, columns] = product

    every = list(range(per_device))
    leading = every[: max(1, per_device - 1)]
    chunk(0, every, True, True)

    @pl.when(all_same)
    def _():
        @pl.loop(1, jnp.maximum(chunks - 1, 1))
        def _(step):
            chunk(step, every, False, False)

        @pl.when(chunks > 1)
        def _():
            chunk(chunks - 1, every, False, True)

    @pl.when(jnp.logical_not(all_same))
    def _():
        @pl.loop(1, jnp.maximum(chunks, 1))
        def _(step):
            chunk(step, leading, False, True)

    for part in every:
        columns = pl.ds(part * rows, rows)
        result = (total_ref[:, columns] / sum_ref[:, columns]).T.astype(out_ref.dtype)
        for at in range(group):
            out_ref[pl.ds(part * block_len, block_len), at * HEAD_SIZE : (at + 1) * HEAD_SIZE] = result[
                at * block_len : (at + 1) * block_len
            ]


def attend(q_base, low, up_rows, kv, place, block_request, block_len, most_blocks, planes):
    tokens, width = q_base.shape
    devices, per_device, rank, span = up_rows.shape
    window = kv.shape[0]
    head_span = width // KEY_VALUE_HEADS
    sources = devices // KEY_VALUE_HEADS
    lanes = tokens * head_span // HEAD_SIZE
    return pl.pallas_call(
        functools.partial(attend_kernel, block_len, most_blocks, planes),
        out_shape=jax.ShapeDtypeStruct((tokens, width), jnp.bfloat16),
        grid_spec=pltpu.PrefetchScalarGridSpec(
            num_scalar_prefetch=2,
            grid=(KEY_VALUE_HEADS,),
            in_specs=[
                pl.BlockSpec((tokens, head_span), lambda m, me, br: (0, m)),
                pl.BlockSpec((rank, tokens), lambda m, me, br: (0, 0)),
                pl.BlockSpec((sources, per_device, rank, span), lambda m, me, br: (m, 0, 0, 0)),
                pl.BlockSpec((window, HEAD_SIZE), lambda m, me, br: (0, m)),
                pl.BlockSpec((window, HEAD_SIZE), lambda m, me, br: (0, KEY_VALUE_HEADS + m)),
            ],
            out_specs=pl.BlockSpec((tokens, head_span), lambda m, me, br: (0, m)),
            scratch_shapes=[
                pltpu.VMEM((lanes, HEAD_SIZE), jnp.bfloat16),
                pltpu.VMEM((HEAD_SIZE, lanes), jnp.float32),
                pltpu.VMEM((1, lanes), jnp.float32),
                pltpu.VMEM((1, lanes), jnp.float32),
            ],
        ),
        cost_estimate=pl.CostEstimate(
            flops=2 * tokens * width * window, bytes_accessed=16 << 20, transcendentals=8 << 20
        ),
        name="attend",
    )(place, block_request, q_base, low, up_rows, kv, kv)


def body(
    hidden,
    q_base,
    base_key_weight,
    base_value_weight,
    shrink_a,
    expand_q,
    key_value_up_weight,
    block_request,
    request_adapter,
):
    tokens = hidden.shape[0]
    devices = lax.axis_size("seq")
    me = lax.axis_index("seq")
    place = me.astype(jnp.int32).reshape(1)
    block_count = block_request.shape[0]
    block_len = tokens * devices // block_count
    per_device = tokens // block_len
    most_blocks = min(MOST_BLOCKS_CAP, block_count // 2)
    hops = -(-(most_blocks - 1) // (PLANE * per_device))
    planes = hops + 1
    chips = devices // CORES
    same_core = [[chip * CORES + core for chip in range(chips)] for core in range(CORES)]
    forward = [(i, i + PLANE) for i in range(devices - PLANE)]
    swap_row = [(i, i ^ CORES) for i in range(devices)]
    swap_core = [(i, i ^ 1) for i in range(devices)]

    sent, kv = split(hidden, base_key_weight, base_value_weight, chips)
    rows = lax.all_to_all(sent, "seq", split_axis=0, concat_axis=0, axis_index_groups=same_core, tiled=True)
    down = jnp.swapaxes(shrink_a, 1, 2)
    other_down = lax.ppermute(down, "seq", swap_core)

    pieces = []
    own = kv
    for back in range(planes):
        if back > 0:
            own = lax.ppermute(own, "seq", forward)
        across = lax.ppermute(own, "seq", swap_row)
        pieces += [
            own,
            lax.ppermute(own, "seq", swap_core),
            across,
            lax.ppermute(across, "seq", swap_core),
        ]

    partials = shrink(rows, down, other_down, place, block_request, request_adapter, block_len)
    received = lax.all_to_all(
        partials, "seq", split_axis=0, concat_axis=0, axis_index_groups=same_core, tiled=True
    )

    adapter_of = request_adapter[block_request]
    picked = expand_q[adapter_of].reshape(devices, per_device, ADAPTER_RANK, expand_q.shape[2])
    up_rows = lax.all_to_all(picked, "seq", split_axis=0, concat_axis=0, tiled=True)

    low = jnp.sum(received.astype(jnp.float32), axis=0).astype(jnp.bfloat16)
    steps = [low[ADAPTER_RANK:]]
    for _ in range(hops):
        steps.append(lax.ppermute(steps[-1], "seq", forward))
    column = jnp.stack(steps)
    both = jnp.concatenate([column, lax.ppermute(column, "seq", swap_row)])
    flipped = lax.ppermute(both, "seq", swap_core)
    lows = jnp.stack([both[:planes], flipped[:planes], both[planes:], flipped[planes:]], axis=1)
    lows = lows.reshape(planes * PLANE, 2 * ADAPTER_RANK, tokens)

    window = finish(
        pieces, lows, key_value_up_weight, place, block_request, request_adapter, block_len, planes
    )
    return attend(
        q_base, low[:ADAPTER_RANK], up_rows, window, place, block_request, block_len, most_blocks, planes
    )


def solution(mesh):
    return jax.shard_map(
        body,
        mesh=mesh,
        in_specs=(
            P(("groups", "seq"), None),
            P(("groups", "seq"), None),
            P(("groups", "seq"), None),
            P(("groups", "seq"), None),
            P("groups", "seq", None),
            P("groups", None, "seq"),
            P("groups", None, None),
            P("groups"),
            P("groups"),
        ),
        out_specs=P(("groups", "seq"), None),
        check_vma=False,
    )
```

time: 375 us -> 253 us (0.67)
  blocking collectives: 117 us -> 0 us
  waiting for transfers between devices: 50.1 us -> 146 us
  local copies, waits for them, and re-layouts: 72.3 us -> 9.18 us
  Pallas kernels: 0 us -> 54.7 us
  other arithmetic: 49.8 us -> 0.79 us
  matrix products: 44.2 us -> 0 us
  starting transfers between devices: 33.5 us -> 41.1 us
    ppermute x0 -> x16, waiting for transfers between devices: none -> 103 us  [the longest x2 54.5 us: body(): own = lax.ppermute(own, 'seq', forward)]
    psum x1 -> x0, blocking collectives: 65.3 us -> none  [body(): shrunk = lax.psum(partial_value, 'seq').astype(jnp.bfloat16)]
    pallas_call x0 -> x4, Pallas kernels: none -> 54.7 us  [the longest x1 32.8 us: attend(): pl.pallas_call(functools.partial(attend_kernel, block_len, most_blocks, p...]
    all_to_all x1 -> x0, blocking collectives: 51.9 us -> none  [body(): lax.all_to_all(head_rows, 'seq', split_axis=0, concat_axis=1, tiled=True)]
    dot_general x11 -> x0, matrix products: 44.2 us -> none  [the longest x4 22.5 us: attend(): jnp.einsum('hqk,kd->qhd', probs, v_rows, preferred_element_type=jnp.float32)]
    sub x4 -> x0, other arithmetic: 35.6 us -> none  [attend(): weights = jnp.exp(scores - row_max)]
    ppermute x0 -> x16, starting transfers between devices: none -> 19.4 us  [the longest x2 4.99 us: body(): own = lax.ppermute(own, 'seq', forward)]
    reshape x7 -> x0, local copies, waits for them, and re-layouts: 16 us -> none  [the longest x2 10.6 us: body(): q_delta = jnp.einsum('btr,brc->btc', low_blocks[:, :, 0], expand_q[adapte...]
  transfers between devices with their start and end apart: 4 -> 19, of which waited for: 2 -> 8; matrix products, arithmetic and copies ran while one was open for 19% -> 3% of each run, Pallas kernels for 0% -> 4%
where the time goes in v1:
time: 253 us; the launch traced here: 252 us
  waiting for transfers between devices  146 us (58%)
  Pallas kernels  54.7 us (22%)
  starting transfers between devices  41.1 us (16%)
  local copies, waits for them, and re-layouts  9.18 us (4%)
    ppermute x2, waiting for transfers between devices, body(): own = lax.ppermute(own, 'seq', forward)  54.5 us
    all_to_all x1, waiting for transfers between devices, body(): lax.all_to_all(sent, 'seq', split_axis=0, concat_axis=0, axis_index_group...  37.9 us
    pallas_call x1, Pallas kernels, attend(): pl.pallas_call(functools.partial(attend_kernel, block_len, most_blocks, p...  32.8 us
    ppermute x1, waiting for transfers between devices, body(): both = jnp.concatenate([column, lax.ppermute(column, 'seq', swap_row)])  31.5 us
    ppermute x2, waiting for transfers between devices, body(): steps.append(lax.ppermute(steps[-1], 'seq', forward))  10.1 us
    pallas_call x1, Pallas kernels, finish(): pl.pallas_call(functools.partial(finish_kernel, block_len, planes), out_s...  9.07 us
    all_to_all x1, starting transfers between devices, body(): lax.all_to_all(picked, 'seq', split_axis=0, concat_axis=0, tiled=True)  8.84 us
    all_to_all x1, starting transfers between devices, body(): lax.all_to_all(partials, 'seq', split_axis=0, concat_axis=0, axis_index_g...  7.26 us
  transfers between devices with their start and end apart: 19, of which 8 were waited for; matrix products, arithmetic and copies ran while one was open for 3% of the time, Pallas kernels for 4%

profile of v1, /device:TPU:23, one launch (start us, length us, event | category | flops | bytes accessed | tf_op | source)
XLA Modules:
  0.0 251.7 jit_solution(15481750746986313374)
XLA Ops:
  0.0 0.0 copy-start
  0.0 6.1 %split.1 = (bf16[8,128,1024]{2,1,0:T(8,128)(2,1)}, bf16[128,2048]{1,0:T(8,128)(2,1)}) custom-call(bf16[128,8192]{1,0:T(8,128)(2,1)} %hidden_ref.1, bf16[128,1024]{1,0:T(8,128)(2,1)} %key_ref.1, bf16[128,1024]{1,0:T(8,128)(2,1)} %value_ref.1), custom_call_target="tpu_custom_call" | custom-call | tf_op jit(solution)/shard_map/split/pallas_call | solution.py:36
  6.1 5.6 %all-to-all-start = ((bf16[8,128,1024]{2,1,0:T(8,128)(2,1)}), bf16[8,128,1024]{2,1,0:T(8,128)(2,1)S(1)}, u32[]{:S(2)}, u32[]{:S(2)}) async-start(bf16[8,128,1024]{2,1,0:T(8,128)(2,1)} %get-tuple-element.7), calls=%async_computation | async-start | bytes 4194304 | tf_op jit(solution)/shard_map/all_to_all | solution.py:341
  11.7 1.2 collective-permute-start
  12.9 5.6 %collective-permute-done.other_ref = bf16[16,192,512]{2,1,0:T(8,128)(2,1)} collective-permute-done((bf16[16,192,512]{2,1,0:T(8,128)(2,1)}, bf16[16,192,512]{2,1,0:T(8,128)(2,1)}, u32[]{:S(2)}, u32[]{:S(2)}) %collective-permute-start) | collective-permute-done | bytes 3145760 | tf_op jit(solution)/shard_map/ppermute | solution.py:343
  18.5 37.9 %all-to-all-done.rows_ref = bf16[8,128,1024]{2,1,0:T(8,128)(2,1)S(1)} async-done(((bf16[8,128,1024]{2,1,0:T(8,128)(2,1)}), bf16[8,128,1024]{2,1,0:T(8,128)(2,1)S(1)}, u32[]{:S(2)}, u32[]{:S(2)}) %all-to-all-start) | async-done | bytes 2097184 | tf_op jit(solution)/shard_map/all_to_all | solution.py:341
  56.5 1.3 copy-done.2
  57.8 6.8 %shrink.1 = bf16[8,192,128]{2,1,0:T(8,128)(2,1)} custom-call(s32[1]{0:T(128)} %bitcast.place_ref, s32[32]{0:T(128)} %request_ref.5, s32[8]{0:T(128)} %adapter_ref.3, bf16[8,128,1024]{2,1,0:T(8,128)(2,1)} %copy-done.2, bf16[16,192,512]{2,1,0:T(8,128)(2,1)} %bitcast.20, bf16[16,192,512]{2,1,0:T(8,128)(2,1)} %collective-permute-done.other_ref), custom_call_target="tpu_custom_call" | custom-call | flops 402653184 | bytes 8388608 | tf_op jit(solution)/shard_map/shrink/pallas_call | solution.py:82
  64.5 7.3 %all-to-all-start.1 = ((bf16[8,192,128]{2,1,0:T(8,128)(2,1)}), bf16[8,192,128]{2,1,0:T(8,128)(2,1)S(1)}, u32[]{:S(2)}, u32[]{:S(2)}) async-start(bf16[8,192,128]{2,1,0:T(8,128)(2,1)} %shrink.1), calls=%async_computation.1 | async-start | bytes 786432 | tf_op jit(solution)/shard_map/all_to_all | solution.py:359
  71.8 0.0 copy-done.13
  71.8 0.0 copy-done.1
  71.8 0.7 gather_fusion
  72.5 0.0 copy-done
  72.6 2.0 gather_fusion.1
  74.6 4.6 %all-to-all-done.1 = bf16[8,192,128]{2,1,0:T(8,128)(2,1)S(1)} async-done(((bf16[8,192,128]{2,1,0:T(8,128)(2,1)}), bf16[8,192,128]{2,1,0:T(8,128)(2,1)S(1)}, u32[]{:S(2)}, u32[]{:S(2)}) %all-to-all-start.1) | async-done | bytes 393248 | tf_op jit(solution)/shard_map/all_to_all | solution.py:359
  79.1 8.8 %all-to-all-start.2 = ((bf16[16,2,64,512]{3,2,1,0:T(8,128)(2,1)}), bf16[16,2,64,512]{3,2,1,0:T(8,128)(2,1)S(1)}, u32[]{:S(2)}, u32[]{:S(2)}) async-start(bf16[16,2,64,512]{3,2,1,0:T(8,128)(2,1)} %bitcast.4), calls=%async_computation.2 | async-start | bytes 4194304 | tf_op jit(solution)/shard_map/all_to_all | solution.py:365
  88.0 3.1 %collective-permute-start.8 = (bf16[128,2048]{1,0:T(8,128)(2,1)}, bf16[128,2048]{1,0:T(8,128)(2,1)}, u32[]{:S(2)}, u32[]{:S(2)}) collective-permute-start(bf16[128,2048]{1,0:T(8,128)(2,1)} %get-tuple-element.8.rest_0_), channel_id=1, source_target_pairs={{0,4},{1,5},{2,6},{3,7},{4,8},{5,9},{6,10},{7,11},{8,12},{9,13},{1... | collective-permute-start | bytes 1572872 | tf_op jit(solution)/shard_map/ppermute | solution.py:349
  91.1 54.5 %collective-permute-done.8.rest_4_ = bf16[128,2048]{1,0:T(8,128)(2,1)} collective-permute-done((bf16[128,2048]{1,0:T(8,128)(2,1)}, bf16[128,2048]{1,0:T(8,128)(2,1)}, u32[]{:S(2)}, u32[]{:S(2)}) %collective-permute-start.8) | collective-permute-done | bytes 524320 | tf_op jit(solution)/shard_map/ppermute | solution.py:349
  145.5 1.9 collective-permute-start.12
  147.5 0.7 reduce_sum.12
  148.1 0.8 slice_bitcast_fusion.2
  148.9 1.9 collective-permute-start.1
  150.8 10.1 %collective-permute-done.1 = bf16[128,128]{1,0:T(8,128)(2,1)S(1)} collective-permute-done((bf16[128,128]{1,0:T(8,128)(2,1)S(1)}, bf16[128,128]{1,0:T(8,128)(2,1)S(1)}, u32[]{:S(2)}, u32[]{:S(2)}) %collective-permute-start.1) | collective-permute-done | bytes 32800 | tf_op jit(solution)/shard_map/ppermute | solution.py:370
  161.0 2.2 collective-permute-start.2
  163.2 0.3 collective-permute-start.6
  163.5 2.0 collective-permute-start.5
  165.5 1.2 collective-permute-start.10
  166.7 0.0 collective-permute-done.12.rest_8_
  166.7 0.3 collective-permute-start.14
  167.0 0.0 collective-permute-done.2
  167.0 1.3 collective-permute-start.3
  168.2 31.5 %collective-permute-done.3 = bf16[3,128,128]{2,1,0:T(8,128)(2,1)S(1)} collective-permute-done((bf16[3,128,128]{2,1,0:T(8,128)(2,1)S(1)}, bf16[3,128,128]{2,1,0:T(8,128)(2,1)S(1)}, u32[]{:S(2)}, u32[]{:S(2)}) %collective-permute-start.3) | collective-permute-done | bytes 98336 | tf_op jit(solution)/shard_map/ppermute | solution.py:372
  199.8 2.6 %collective-permute-start.4 = (bf16[6,128,128]{2,1,0:T(8,128)(2,1)S(1)}, bf16[6,128,128]{2,1,0:T(8,128)(2,1)S(1)}, u32[]{:S(2)}, u32[]{:S(2)}) collective-permute-start(bf16[6,128,128]{2,1,0:T(8,128)(2,1)S(1)} %pad_maximum_fusion.1), channel_id=1, source_target_pairs={{0,1},{1,0},{2,3},{3,2},{4,5},{5,4},{6,7},{7,6},{8,9},{9,8},{10,11... | collective-permute-start | bytes 589832 | tf_op jit(solution)/shard_map/ppermute | solution.py:373
  202.4 0.0 collective-permute-done.6.rest_2_
  202.4 0.1 collective-permute-start.9
  202.5 0.0 collective-permute-done.5.rest_1_
  202.5 0.4 collective-permute-start.7
  203.0 0.0 collective-permute-done.10.rest_6_
  203.0 0.1 collective-permute-start.13
  203.1 0.0 collective-permute-done.14.rest_10_
  203.1 0.4 collective-permute-start.11
  203.5 0.0 collective-permute-done.4
  203.5 0.4 collective-permute-start.15
  203.9 1.3 slice.20.low_ref
  205.2 0.0 copy-done.5
  205.2 0.1 pad_maximum_fusion
  205.3 0.8 copy.10
  206.1 0.0 copy-done.4
  206.1 0.0 collective-permute-done.9.rest_5_
  206.1 0.0 collective-permute-done.7.rest_3_
  206.1 0.0 copy-done.6
  206.1 0.0 copy-start.9
  206.1 0.0 collective-permute-done.13.rest_9_
  206.1 0.0 copy-start.10
  206.1 0.7 collective-permute-done.11.rest_7_
  206.8 0.0 copy-done.7
  206.8 0.7 collective-permute-done.15.rest_11_
  207.6 0.0 copy-done.8
  207.6 0.0 copy-done.11
  207.6 0.8 copy-done.12
  208.4 9.1 %finish.1.key_ref.value_ref = bf16[1536,2048]{1,0:T(8,128)(2,1)} custom-call(s32[1]{0:T(128)} %bitcast.place_ref, s32[32]{0:T(128)} %request_ref.5, s32[8]{0:T(128)} %adapter_ref.3, bf16[12,128,128]{2,1,0:T(8,128)(2,1)} %bitcast.21, bf16[16,64,2048]{2,1,0:T(8,128)(2,1)} %up_ref.1, bf16[128,2048]{1,0:T(8,128)(2,1)} %get-tuple-element.8.rest_0_, ...), custom_call_target="tpu_custom_call" | custom-call | flops 402653184 | bytes 12582912 | tf_op jit(solution)/shard_map/finish/pallas_call | solution.py:146
  217.5 0.0 all-to-all-done.2.up_ref
  217.5 1.4 copy-done.3
  218.9 32.8 %attend.1 = bf16[128,8192]{1,0:T(8,128)(2,1)} custom-call(s32[1]{0:T(128)} %bitcast.place_ref, s32[32]{0:T(128)} %request_ref.5, bf16[128,8192]{1,0:T(8,128)(2,1)} %q_ref.1, bf16[64,128]{1,0:T(8,128)(2,1)} %slice.20.low_ref, bf16[16,2,64,512]{3,2,1,0:T(8,128)(2,1)} %copy-done.3, bf16[1536,2048]{1,0:T(8,128)(2,1)} %finish.1.key_ref.value_ref, ...), custom_call_target="tpu_custom_call" | custom-call | flops 3221225472 | bytes 16777216 | tf_op jit(solution)/shard_map/attend/pallas_call | solution.py:285
  (20 shorter events, 0.1 us)
Async XLA Ops:
  0.0 72.5 %copy-start = (bf16[16,64,512]{2,1,0:T(8,128)(2,1)S(1)}, bf16[16,64,512]{2,1,0:T(8,128)(2,1)}, u32[]{:S(2)}) copy-start(bf16[16,64,512]{2,1,0:T(8,128)(2,1)} %param.14) | copy-start | bytes 3145732
  6.1 50.4 %all-to-all-start = ((bf16[8,128,1024]{2,1,0:T(8,128)(2,1)}), bf16[8,128,1024]{2,1,0:T(8,128)(2,1)S(1)}, u32[]{:S(2)}, u32[]{:S(2)}) async-start(bf16[8,128,1024]{2,1,0:T(8,128)(2,1)} %get-tuple-element.7), calls=%async_computation | async-start | bytes 4194304 | tf_op jit(solution)/shard_map/all_to_all | solution.py:341
  11.7 6.9 %collective-permute-start = (bf16[16,192,512]{2,1,0:T(8,128)(2,1)}, bf16[16,192,512]{2,1,0:T(8,128)(2,1)}, u32[]{:S(2)}, u32[]{:S(2)}) collective-permute-start(bf16[16,192,512]{2,1,0:T(8,128)(2,1)} %bitcast.19), channel_id=1, source_target_pairs={{0,1},{1,0},{2,3},{3,2},{4,5},{5,4},{6,7},{7,6},{8,9},{9,8},{10,11... | collective-permute-start | bytes 9437192 | tf_op jit(solution)/shard_map/ppermute | solution.py:343
  56.5 1.3 copy-start.2
  57.8 14.0 %copy-start.13 = (s32[32]{0:T(128)S(1)}, s32[32]{0:T(128)}, u32[]{:S(2)}) copy-start(s32[32]{0:T(128)} %request_ref.5) | copy-start | bytes 388
  57.8 14.0 %copy-start.1 = (s32[8]{0:T(128)S(1)}, s32[8]{0:T(128)}, u32[]{:S(2)}) copy-start(s32[8]{0:T(128)} %adapter_ref.3) | copy-start | bytes 100
  64.5 14.6 %all-to-all-start.1 = ((bf16[8,192,128]{2,1,0:T(8,128)(2,1)}), bf16[8,192,128]{2,1,0:T(8,128)(2,1)S(1)}, u32[]{:S(2)}, u32[]{:S(2)}) async-start(bf16[8,192,128]{2,1,0:T(8,128)(2,1)} %shrink.1), calls=%async_computation.1 | async-start | bytes 786432 | tf_op jit(solution)/shard_map/all_to_all | solution.py:359
  79.1 138.4 %all-to-all-start.2 = ((bf16[16,2,64,512]{3,2,1,0:T(8,128)(2,1)}), bf16[16,2,64,512]{3,2,1,0:T(8,128)(2,1)S(1)}, u32[]{:S(2)}, u32[]{:S(2)}) async-start(bf16[16,2,64,512]{3,2,1,0:T(8,128)(2,1)} %bitcast.4), calls=%async_computation.2 | async-start | bytes 4194304 | tf_op jit(solution)/shard_map/all_to_all | solution.py:365
  88.0 57.6 %collective-permute-start.8 = (bf16[128,2048]{1,0:T(8,128)(2,1)}, bf16[128,2048]{1,0:T(8,128)(2,1)}, u32[]{:S(2)}, u32[]{:S(2)}) collective-permute-start(bf16[128,2048]{1,0:T(8,128)(2,1)} %get-tuple-element.8.rest_0_), channel_id=1, source_target_pairs={{0,4},{1,5},{2,6},{3,7},{4,8},{5,9},{6,10},{7,11},{8,12},{9,13},{1... | collective-permute-start | bytes 1572872 | tf_op jit(solution)/shard_map/ppermute | solution.py:349
  145.5 21.1 %collective-permute-start.12 = (bf16[128,2048]{1,0:T(8,128)(2,1)}, bf16[128,2048]{1,0:T(8,128)(2,1)}, u32[]{:S(2)}, u32[]{:S(2)}) collective-permute-start(bf16[128,2048]{1,0:T(8,128)(2,1)} %collective-permute-done.8.rest_4_), channel_id=1, source_target_pairs={{0,4},{1,5},{2,6},{3,7},{4,8},{5,9},{6,10},{7,11},{8,12},{9,13},{1... | collective-permute-start | bytes 1572872 | tf_op jit(solution)/shard_map/ppermute | solution.py:349
  148.9 12.1 %collective-permute-start.1 = (bf16[128,128]{1,0:T(8,128)(2,1)S(1)}, bf16[128,128]{1,0:T(8,128)(2,1)S(1)}, u32[]{:S(2)}, u32[]{:S(2)}) collective-permute-start(bf16[128,128]{1,0:T(8,128)(2,1)S(1)} %get-tuple-element.14), channel_id=1, source_target_pairs={{0,4},{1,5},{2,6},{3,7},{4,8},{5,9},{6,10},{7,11},{8,12},{9,13},{1... | collective-permute-start | bytes 98312 | tf_op jit(solution)/shard_map/ppermute | solution.py:370
  161.0 6.0 %collective-permute-start.2 = (bf16[128,128]{1,0:T(8,128)(2,1)S(1)}, bf16[128,128]{1,0:T(8,128)(2,1)S(1)}, u32[]{:S(2)}, u32[]{:S(2)}) collective-permute-start(bf16[128,128]{1,0:T(8,128)(2,1)S(1)} %collective-permute-done.1), channel_id=1, source_target_pairs={{0,4},{1,5},{2,6},{3,7},{4,8},{5,9},{6,10},{7,11},{8,12},{9,13},{1... | collective-permute-start | bytes 98312 | tf_op jit(solution)/shard_map/ppermute | solution.py:370
  163.2 39.3 %collective-permute-start.6 = (bf16[128,2048]{1,0:T(8,128)(2,1)}, bf16[128,2048]{1,0:T(8,128)(2,1)S(1)}, u32[]{:S(2)}, u32[]{:S(2)}) collective-permute-start(bf16[128,2048]{1,0:T(8,128)(2,1)} %get-tuple-element.8.rest_0_), channel_id=1, source_target_pairs={{0,2},{1,3},{2,0},{3,1},{4,6},{5,7},{6,4},{7,5},{8,10},{9,11},{10,... | collective-permute-start | bytes 1572872 | tf_op jit(solution)/shard_map/ppermute | solution.py:350
  163.5 39.0 %collective-permute-start.5 = (bf16[128,2048]{1,0:T(8,128)(2,1)}, bf16[128,2048]{1,0:T(8,128)(2,1)S(1)}, u32[]{:S(2)}, u32[]{:S(2)}) collective-permute-start(bf16[128,2048]{1,0:T(8,128)(2,1)} %get-tuple-element.8.rest_0_), channel_id=1, source_target_pairs={{0,1},{1,0},{2,3},{3,2},{4,5},{5,4},{6,7},{7,6},{8,9},{9,8},{10,11... | collective-permute-start | bytes 1572872 | tf_op jit(solution)/shard_map/ppermute | solution.py:353
  165.5 37.5 %collective-permute-start.10 = (bf16[128,2048]{1,0:T(8,128)(2,1)}, bf16[128,2048]{1,0:T(8,128)(2,1)S(1)}, u32[]{:S(2)}, u32[]{:S(2)}) collective-permute-start(bf16[128,2048]{1,0:T(8,128)(2,1)} %collective-permute-done.8.rest_4_), channel_id=1, source_target_pairs={{0,2},{1,3},{2,0},{3,1},{4,6},{5,7},{6,4},{7,5},{8,10},{9,11},{10,... | collective-permute-start | bytes 1572872 | tf_op jit(solution)/shard_map/ppermute | solution.py:350
  166.7 36.4 %collective-permute-start.14 = (bf16[128,2048]{1,0:T(8,128)(2,1)}, bf16[128,2048]{1,0:T(8,128)(2,1)S(1)}, u32[]{:S(2)}, u32[]{:S(2)}) collective-permute-start(bf16[128,2048]{1,0:T(8,128)(2,1)} %collective-permute-done.12.rest_8_), channel_id=1, source_target_pairs={{0,2},{1,3},{2,0},{3,1},{4,6},{5,7},{6,4},{7,5},{8,10},{9,11},{10,... | collective-permute-start | bytes 1572872 | tf_op jit(solution)/shard_map/ppermute | solution.py:350
  167.0 32.8 %collective-permute-start.3 = (bf16[3,128,128]{2,1,0:T(8,128)(2,1)S(1)}, bf16[3,128,128]{2,1,0:T(8,128)(2,1)S(1)}, u32[]{:S(2)}, u32[]{:S(2)}) collective-permute-start(bf16[3,128,128]{2,1,0:T(8,128)(2,1)S(1)} %get-tuple-element.12), channel_id=1, source_target_pairs={{0,2},{1,3},{2,0},{3,1},{4,6},{5,7},{6,4},{7,5},{8,10},{9,11},{10,... | collective-permute-start | bytes 294920 | tf_op jit(solution)/shard_map/ppermute | solution.py:372
  199.8 3.7 %collective-permute-start.4 = (bf16[6,128,128]{2,1,0:T(8,128)(2,1)S(1)}, bf16[6,128,128]{2,1,0:T(8,128)(2,1)S(1)}, u32[]{:S(2)}, u32[]{:S(2)}) collective-permute-start(bf16[6,128,128]{2,1,0:T(8,128)(2,1)S(1)} %pad_maximum_fusion.1), channel_id=1, source_target_pairs={{0,1},{1,0},{2,3},{3,2},{4,5},{5,4},{6,7},{7,6},{8,9},{9,8},{10,11... | collective-permute-start | bytes 589832 | tf_op jit(solution)/shard_map/ppermute | solution.py:373
  202.4 3.7 %copy-start.4 = (bf16[128,2048]{1,0:T(8,128)(2,1)}, bf16[128,2048]{1,0:T(8,128)(2,1)S(1)}, u32[]{:S(2)}) copy-start(bf16[128,2048]{1,0:T(8,128)(2,1)S(1)} %collective-permute-done.6.rest_2_) | copy-start | bytes 1572868
  202.4 3.7 %collective-permute-start.9 = (bf16[128,2048]{1,0:T(8,128)(2,1)}, bf16[128,2048]{1,0:T(8,128)(2,1)S(1)}, u32[]{:S(2)}, u32[]{:S(2)}) collective-permute-start(bf16[128,2048]{1,0:T(8,128)(2,1)} %collective-permute-done.8.rest_4_), channel_id=1, source_target_pairs={{0,1},{1,0},{2,3},{3,2},{4,5},{5,4},{6,7},{7,6},{8,9},{9,8},{10,11... | collective-permute-start | bytes 1572872 | tf_op jit(solution)/shard_map/ppermute | solution.py:353
  202.5 2.7 %copy-start.5 = (bf16[128,2048]{1,0:T(8,128)(2,1)}, bf16[128,2048]{1,0:T(8,128)(2,1)S(1)}, u32[]{:S(2)}) copy-start(bf16[128,2048]{1,0:T(8,128)(2,1)S(1)} %collective-permute-done.5.rest_1_) | copy-start | bytes 1572868
  202.5 3.6 %collective-permute-start.7 = (bf16[128,2048]{1,0:T(8,128)(2,1)S(1)}, bf16[128,2048]{1,0:T(8,128)(2,1)S(1)}, u32[]{:S(2)}, u32[]{:S(2)}) collective-permute-start(bf16[128,2048]{1,0:T(8,128)(2,1)S(1)} %collective-permute-done.6.rest_2_), channel_id=1, source_target_pairs={{0,1},{1,0},{2,3},{3,2},{4,5},{5,4},{6,7},{7,6},{8,9},{9,8},{10,11... | collective-permute-start | bytes 1572872 | tf_op jit(solution)/shard_map/ppermute | solution.py:355
  203.0 3.1 %copy-start.6 = (bf16[128,2048]{1,0:T(8,128)(2,1)}, bf16[128,2048]{1,0:T(8,128)(2,1)S(1)}, u32[]{:S(2)}) copy-start(bf16[128,2048]{1,0:T(8,128)(2,1)S(1)} %collective-permute-done.10.rest_6_) | copy-start | bytes 1572868
  203.0 3.2 %collective-permute-start.13 = (bf16[128,2048]{1,0:T(8,128)(2,1)}, bf16[128,2048]{1,0:T(8,128)(2,1)S(1)}, u32[]{:S(2)}, u32[]{:S(2)}) collective-permute-start(bf16[128,2048]{1,0:T(8,128)(2,1)} %collective-permute-done.12.rest_8_), channel_id=1, source_target_pairs={{0,1},{1,0},{2,3},{3,2},{4,5},{5,4},{6,7},{7,6},{8,9},{9,8},{10,11... | collective-permute-start | bytes 1572872 | tf_op jit(solution)/shard_map/ppermute | solution.py:353
  203.1 3.8 %copy-start.7 = (bf16[128,2048]{1,0:T(8,128)(2,1)}, bf16[128,2048]{1,0:T(8,128)(2,1)S(1)}, u32[]{:S(2)}) copy-start(bf16[128,2048]{1,0:T(8,128)(2,1)S(1)} %collective-permute-done.14.rest_10_) | copy-start | bytes 1572868
  203.1 3.7 %collective-permute-start.11 = (bf16[128,2048]{1,0:T(8,128)(2,1)S(1)}, bf16[128,2048]{1,0:T(8,128)(2,1)S(1)}, u32[]{:S(2)}, u32[]{:S(2)}) collective-permute-start(bf16[128,2048]{1,0:T(8,128)(2,1)S(1)} %collective-permute-done.10.rest_6_), channel_id=1, source_target_pairs={{0,1},{1,0},{2,3},{3,2},{4,5},{5,4},{6,7},{7,6},{8,9},{9,8},{10,11... | collective-permute-start | bytes 1572872 | tf_op jit(solution)/shard_map/ppermute | solution.py:355
  203.5 4.1 %collective-permute-start.15 = (bf16[128,2048]{1,0:T(8,128)(2,1)S(1)}, bf16[128,2048]{1,0:T(8,128)(2,1)S(1)}, u32[]{:S(2)}, u32[]{:S(2)}) collective-permute-start(bf16[128,2048]{1,0:T(8,128)(2,1)S(1)} %collective-permute-done.14.rest_10_), channel_id=1, source_target_pairs={{0,1},{1,0},{2,3},{3,2},{4,5},{5,4},{6,7},{7,6},{8,9},{9,8},{10,11... | collective-permute-start | bytes 1572872 | tf_op jit(solution)/shard_map/ppermute | solution.py:355
  206.1 1.5 copy-start.8
  206.1 1.5 copy-start.9
  206.1 1.4 copy-start.10
  206.8 0.8 copy-start.11
  207.6 0.8 copy-start.12
  217.5 1.4 copy-start.3

commit v2 on v1

--- a/solution.py
+++ b/solution.py
@@ -338,7 +338,9 @@
     swap_core = [(i, i ^ 1) for i in range(devices)]
 
     sent, kv = split(hidden, base_key_weight, base_value_weight, chips)
-    rows = lax.all_to_all(sent, "seq", split_axis=0, concat_axis=0, axis_index_groups=same_core, tiled=True)
+    rows = lax.all_to_all(
+        sent, "seq", split_axis=0, concat_axis=0, axis_index_groups=same_core, tiled=True
+    )
     down = jnp.swapaxes(shrink_a, 1, 2)
     other_down = lax.ppermute(down, "seq", swap_core)
 
@@ -348,12 +350,9 @@
         if back > 0:
             own = lax.ppermute(own, "seq", forward)
         across = lax.ppermute(own, "seq", swap_row)
-        pieces += [
-            own,
-            lax.ppermute(own, "seq", swap_core),
-            across,
-            lax.ppermute(across, "seq", swap_core),
-        ]
+        flipped = lax.ppermute(own, "seq", swap_core)
+        both = lax.ppermute(across, "seq", swap_core)
+        pieces += [own, flipped, across, both]
 
     partials = shrink(rows, down, other_down, place, block_request, request_adapter, block_len)
     received = lax.all_to_all(
@@ -366,7 +365,7 @@
 
     low = jnp.sum(received.astype(jnp.float32), axis=0).astype(jnp.bfloat16)
     steps = [low[ADAPTER_RANK:]]
-    for _ in range(hops):
+    for _ in range(1, planes):
         steps.append(lax.ppermute(steps[-1], "seq", forward))
     column = jnp.stack(steps)
     both = jnp.concatenate([column, lax.ppermute(column, "seq", swap_row)])

time: 253 us -> 253 us (level)
  the two profiles are of different devices: /device:TPU:23 before, /device:TPU:19 now
where the time goes in v2:
time: 253 us; the launch traced here: 252 us
  waiting for transfers between devices  148 us (58%)
  Pallas kernels  54.7 us (22%)
  starting transfers between devices  39 us (15%)
  local copies, waits for them, and re-layouts  9.18 us (4%)
    ppermute x2, waiting for transfers between devices, body(): own = lax.ppermute(own, 'seq', forward)  54.5 us
    all_to_all x1, waiting for transfers between devices, body(): lax.all_to_all(sent, 'seq', split_axis=0, concat_axis=0, axis_index_group...  37.6 us
    pallas_call x1, Pallas kernels, attend(): pl.pallas_call(functools.partial(attend_kernel, block_len, most_blocks, p...  32.8 us
    ppermute x1, waiting for transfers between devices, body(): both = jnp.concatenate([column, lax.ppermute(column, 'seq', swap_row)])  31.5 us
    ppermute x2, waiting for transfers between devices, body(): steps.append(lax.ppermute(steps[-1], 'seq', forward))  10.1 us
    pallas_call x1, Pallas kernels, finish(): pl.pallas_call(functools.partial(finish_kernel, block_len, planes), out_s...  9.06 us
    all_to_all x1, starting transfers between devices, body(): lax.all_to_all(partials, 'seq', split_axis=0, concat_axis=0, axis_index_g...  7.62 us
    all_to_all x1, waiting for transfers between devices, body(): lax.all_to_all(partials, 'seq', split_axis=0, concat_axis=0, axis_index_g...  7.06 us
  transfers between devices with their start and end apart: 19, of which 8 were waited for; matrix products, arithmetic and copies ran while one was open for 3% of the time, Pallas kernels for 4%

profile of v2, /device:TPU:19, one launch (start us, length us, event | category | flops | bytes accessed | tf_op | source)
XLA Modules:
  0.0 251.7 jit_solution(15481750746986313374)
XLA Ops:
  0.0 0.0 copy-start
  0.0 6.1 %split.1 = (bf16[8,128,1024]{2,1,0:T(8,128)(2,1)}, bf16[128,2048]{1,0:T(8,128)(2,1)}) custom-call(bf16[128,8192]{1,0:T(8,128)(2,1)} %hidden_ref.1, bf16[128,1024]{1,0:T(8,128)(2,1)} %key_ref.1, bf16[128,1024]{1,0:T(8,128)(2,1)} %value_ref.1), custom_call_target="tpu_custom_call" | custom-call | tf_op jit(solution)/shard_map/split/pallas_call | solution.py:36
  6.1 5.6 %all-to-all-start = ((bf16[8,128,1024]{2,1,0:T(8,128)(2,1)}), bf16[8,128,1024]{2,1,0:T(8,128)(2,1)S(1)}, u32[]{:S(2)}, u32[]{:S(2)}) async-start(bf16[8,128,1024]{2,1,0:T(8,128)(2,1)} %get-tuple-element.7), calls=%async_computation | async-start | bytes 4194304 | tf_op jit(solution)/shard_map/all_to_all | solution.py:341
  11.7 1.2 collective-permute-start
  13.0 5.6 %collective-permute-done.other_ref = bf16[16,192,512]{2,1,0:T(8,128)(2,1)} collective-permute-done((bf16[16,192,512]{2,1,0:T(8,128)(2,1)}, bf16[16,192,512]{2,1,0:T(8,128)(2,1)}, u32[]{:S(2)}, u32[]{:S(2)}) %collective-permute-start) | collective-permute-done | bytes 3145760 | tf_op jit(solution)/shard_map/ppermute | solution.py:345
  18.6 37.6 %all-to-all-done.rows_ref = bf16[8,128,1024]{2,1,0:T(8,128)(2,1)S(1)} async-done(((bf16[8,128,1024]{2,1,0:T(8,128)(2,1)}), bf16[8,128,1024]{2,1,0:T(8,128)(2,1)S(1)}, u32[]{:S(2)}, u32[]{:S(2)}) %all-to-all-start) | async-done | bytes 2097184 | tf_op jit(solution)/shard_map/all_to_all | solution.py:341
  56.2 1.3 copy-done.2
  57.5 6.8 %shrink.1 = bf16[8,192,128]{2,1,0:T(8,128)(2,1)} custom-call(s32[1]{0:T(128)} %bitcast.place_ref, s32[32]{0:T(128)} %request_ref.5, s32[8]{0:T(128)} %adapter_ref.3, bf16[8,128,1024]{2,1,0:T(8,128)(2,1)} %copy-done.2, bf16[16,192,512]{2,1,0:T(8,128)(2,1)} %bitcast.20, bf16[16,192,512]{2,1,0:T(8,128)(2,1)} %collective-permute-done.other_ref), custom_call_target="tpu_custom_call" | custom-call | flops 402653184 | bytes 8388608 | tf_op jit(solution)/shard_map/shrink/pallas_call | solution.py:82
  64.2 7.6 %all-to-all-start.1 = ((bf16[8,192,128]{2,1,0:T(8,128)(2,1)}), bf16[8,192,128]{2,1,0:T(8,128)(2,1)S(1)}, u32[]{:S(2)}, u32[]{:S(2)}) async-start(bf16[8,192,128]{2,1,0:T(8,128)(2,1)} %shrink.1), calls=%async_computation.1 | async-start | bytes 786432 | tf_op jit(solution)/shard_map/all_to_all | solution.py:358
  71.9 0.0 copy-done.13
  71.9 0.0 copy-done.1
  71.9 0.7 gather_fusion
  72.6 0.0 copy-done
  72.6 2.0 gather_fusion.1
  74.6 7.1 %all-to-all-done.1 = bf16[8,192,128]{2,1,0:T(8,128)(2,1)S(1)} async-done(((bf16[8,192,128]{2,1,0:T(8,128)(2,1)}), bf16[8,192,128]{2,1,0:T(8,128)(2,1)S(1)}, u32[]{:S(2)}, u32[]{:S(2)}) %all-to-all-start.1) | async-done | bytes 393248 | tf_op jit(solution)/shard_map/all_to_all | solution.py:358
  81.7 6.4 %all-to-all-start.2 = ((bf16[16,2,64,512]{3,2,1,0:T(8,128)(2,1)}), bf16[16,2,64,512]{3,2,1,0:T(8,128)(2,1)S(1)}, u32[]{:S(2)}, u32[]{:S(2)}) async-start(bf16[16,2,64,512]{3,2,1,0:T(8,128)(2,1)} %bitcast.4), calls=%async_computation.2 | async-start | bytes 4194304 | tf_op jit(solution)/shard_map/all_to_all | solution.py:364
  88.0 3.1 %collective-permute-start.8 = (bf16[128,2048]{1,0:T(8,128)(2,1)}, bf16[128,2048]{1,0:T(8,128)(2,1)}, u32[]{:S(2)}, u32[]{:S(2)}) collective-permute-start(bf16[128,2048]{1,0:T(8,128)(2,1)} %get-tuple-element.8.rest_0_), channel_id=1, source_target_pairs={{0,4},{1,5},{2,6},{3,7},{4,8},{5,9},{6,10},{7,11},{8,12},{9,13},{1... | collective-permute-start | bytes 1572872 | tf_op jit(solution)/shard_map/ppermute | solution.py:351
  91.1 54.5 %collective-permute-done.8.rest_4_ = bf16[128,2048]{1,0:T(8,128)(2,1)} collective-permute-done((bf16[128,2048]{1,0:T(8,128)(2,1)}, bf16[128,2048]{1,0:T(8,128)(2,1)}, u32[]{:S(2)}, u32[]{:S(2)}) %collective-permute-start.8) | collective-permute-done | bytes 524320 | tf_op jit(solution)/shard_map/ppermute | solution.py:351
  145.6 1.9 collective-permute-start.12
  147.5 0.7 reduce_sum.12
  148.2 0.8 slice_bitcast_fusion.2
  148.9 1.9 collective-permute-start.1
  150.9 10.1 %collective-permute-done.1 = bf16[128,128]{1,0:T(8,128)(2,1)S(1)} collective-permute-done((bf16[128,128]{1,0:T(8,128)(2,1)S(1)}, bf16[128,128]{1,0:T(8,128)(2,1)S(1)}, u32[]{:S(2)}, u32[]{:S(2)}) %collective-permute-start.1) | collective-permute-done | bytes 32800 | tf_op jit(solution)/shard_map/ppermute | solution.py:369
  161.0 2.2 collective-permute-start.2
  163.2 1.3 collective-permute-start.6
  164.5 2.0 collective-permute-start.5
  166.5 0.3 collective-permute-start.10
  166.7 0.0 collective-permute-done.12.rest_8_
  166.7 1.2 collective-permute-start.14
  167.9 0.0 collective-permute-done.2
  168.0 0.3 collective-permute-start.3
  168.3 31.5 %collective-permute-done.3 = bf16[3,128,128]{2,1,0:T(8,128)(2,1)S(1)} collective-permute-done((bf16[3,128,128]{2,1,0:T(8,128)(2,1)S(1)}, bf16[3,128,128]{2,1,0:T(8,128)(2,1)S(1)}, u32[]{:S(2)}, u32[]{:S(2)}) %collective-permute-start.3) | collective-permute-done | bytes 98336 | tf_op jit(solution)/shard_map/ppermute | solution.py:371
  199.8 2.6 %collective-permute-start.4 = (bf16[6,128,128]{2,1,0:T(8,128)(2,1)S(1)}, bf16[6,128,128]{2,1,0:T(8,128)(2,1)S(1)}, u32[]{:S(2)}, u32[]{:S(2)}) collective-permute-start(bf16[6,128,128]{2,1,0:T(8,128)(2,1)S(1)} %pad_maximum_fusion.1), channel_id=1, source_target_pairs={{0,1},{1,0},{2,3},{3,2},{4,5},{5,4},{6,7},{7,6},{8,9},{9,8},{10,11... | collective-permute-start | bytes 589832 | tf_op jit(solution)/shard_map/ppermute | solution.py:372
  202.5 0.0 collective-permute-done.6.rest_2_
  202.5 0.1 collective-permute-start.9
  202.6 0.0 collective-permute-done.5.rest_1_
  202.6 0.4 collective-permute-start.7
  203.0 0.0 collective-permute-done.10.rest_6_
  203.0 0.1 collective-permute-start.13
  203.1 0.0 collective-permute-done.14.rest_10_
  203.1 0.4 collective-permute-start.11
  203.5 0.0 collective-permute-done.4
  203.6 0.4 collective-permute-start.15
  203.9 1.3 slice.20.low_ref
  205.3 0.0 copy-done.5
  205.3 0.1 pad_maximum_fusion
  205.3 0.8 copy.10
  206.1 0.0 copy-done.4
  206.1 0.0 collective-permute-done.9.rest_5_
  206.1 0.0 collective-permute-done.7.rest_3_
  206.2 0.0 copy-done.6
  206.2 0.0 copy-start.9
  206.2 0.0 collective-permute-done.13.rest_9_
  206.2 0.0 copy-start.10
  206.2 0.7 collective-permute-done.11.rest_7_
  206.9 0.0 copy-done.7
  206.9 0.7 collective-permute-done.15.rest_11_
  207.6 0.0 copy-done.9
  207.6 0.0 copy-done.11
  207.6 0.8 copy-done.12
  208.5 9.1 %finish.1.key_ref.value_ref = bf16[1536,2048]{1,0:T(8,128)(2,1)} custom-call(s32[1]{0:T(128)} %bitcast.place_ref, s32[32]{0:T(128)} %request_ref.5, s32[8]{0:T(128)} %adapter_ref.3, bf16[12,128,128]{2,1,0:T(8,128)(2,1)} %bitcast.21, bf16[16,64,2048]{2,1,0:T(8,128)(2,1)} %up_ref.1, bf16[128,2048]{1,0:T(8,128)(2,1)} %get-tuple-element.8.rest_0_, ...), custom_call_target="tpu_custom_call" | custom-call | flops 402653184 | bytes 12582912 | tf_op jit(solution)/shard_map/finish/pallas_call | solution.py:146
  217.5 0.0 all-to-all-done.2.up_ref
  217.5 1.4 copy-done.3
  218.9 32.8 %attend.1 = bf16[128,8192]{1,0:T(8,128)(2,1)} custom-call(s32[1]{0:T(128)} %bitcast.place_ref, s32[32]{0:T(128)} %request_ref.5, bf16[128,8192]{1,0:T(8,128)(2,1)} %q_ref.1, bf16[64,128]{1,0:T(8,128)(2,1)} %slice.20.low_ref, bf16[16,2,64,512]{3,2,1,0:T(8,128)(2,1)} %copy-done.3, bf16[1536,2048]{1,0:T(8,128)(2,1)} %finish.1.key_ref.value_ref, ...), custom_call_target="tpu_custom_call" | custom-call | flops 3221225472 | bytes 16777216 | tf_op jit(solution)/shard_map/attend/pallas_call | solution.py:285
  (20 shorter events, 0.1 us)
Async XLA Ops:
  0.0 72.6 %copy-start = (bf16[16,64,512]{2,1,0:T(8,128)(2,1)S(1)}, bf16[16,64,512]{2,1,0:T(8,128)(2,1)}, u32[]{:S(2)}) copy-start(bf16[16,64,512]{2,1,0:T(8,128)(2,1)} %param.14) | copy-start | bytes 3145732
  6.1 50.0 %all-to-all-start = ((bf16[8,128,1024]{2,1,0:T(8,128)(2,1)}), bf16[8,128,1024]{2,1,0:T(8,128)(2,1)S(1)}, u32[]{:S(2)}, u32[]{:S(2)}) async-start(bf16[8,128,1024]{2,1,0:T(8,128)(2,1)} %get-tuple-element.7), calls=%async_computation | async-start | bytes 4194304 | tf_op jit(solution)/shard_map/all_to_all | solution.py:341
  11.7 6.9 %collective-permute-start = (bf16[16,192,512]{2,1,0:T(8,128)(2,1)}, bf16[16,192,512]{2,1,0:T(8,128)(2,1)}, u32[]{:S(2)}, u32[]{:S(2)}) collective-permute-start(bf16[16,192,512]{2,1,0:T(8,128)(2,1)} %bitcast.19), channel_id=1, source_target_pairs={{0,1},{1,0},{2,3},{3,2},{4,5},{5,4},{6,7},{7,6},{8,9},{9,8},{10,11... | collective-permute-start | bytes 9437192 | tf_op jit(solution)/shard_map/ppermute | solution.py:345
  56.2 1.3 copy-start.2
  57.5 14.4 %copy-start.13 = (s32[32]{0:T(128)S(1)}, s32[32]{0:T(128)}, u32[]{:S(2)}) copy-start(s32[32]{0:T(128)} %request_ref.5) | copy-start | bytes 388
  57.5 14.4 %copy-start.1 = (s32[8]{0:T(128)S(1)}, s32[8]{0:T(128)}, u32[]{:S(2)}) copy-start(s32[8]{0:T(128)} %adapter_ref.3) | copy-start | bytes 100
  64.2 17.4 %all-to-all-start.1 = ((bf16[8,192,128]{2,1,0:T(8,128)(2,1)}), bf16[8,192,128]{2,1,0:T(8,128)(2,1)S(1)}, u32[]{:S(2)}, u32[]{:S(2)}) async-start(bf16[8,192,128]{2,1,0:T(8,128)(2,1)} %shrink.1), calls=%async_computation.1 | async-start | bytes 786432 | tf_op jit(solution)/shard_map/all_to_all | solution.py:358
  81.7 135.9 %all-to-all-start.2 = ((bf16[16,2,64,512]{3,2,1,0:T(8,128)(2,1)}), bf16[16,2,64,512]{3,2,1,0:T(8,128)(2,1)S(1)}, u32[]{:S(2)}, u32[]{:S(2)}) async-start(bf16[16,2,64,512]{3,2,1,0:T(8,128)(2,1)} %bitcast.4), calls=%async_computation.2 | async-start | bytes 4194304 | tf_op jit(solution)/shard_map/all_to_all | solution.py:364
  88.0 57.6 %collective-permute-start.8 = (bf16[128,2048]{1,0:T(8,128)(2,1)}, bf16[128,2048]{1,0:T(8,128)(2,1)}, u32[]{:S(2)}, u32[]{:S(2)}) collective-permute-start(bf16[128,2048]{1,0:T(8,128)(2,1)} %get-tuple-element.8.rest_0_), channel_id=1, source_target_pairs={{0,4},{1,5},{2,6},{3,7},{4,8},{5,9},{6,10},{7,11},{8,12},{9,13},{1... | collective-permute-start | bytes 1572872 | tf_op jit(solution)/shard_map/ppermute | solution.py:351
  145.6 21.1 %collective-permute-start.12 = (bf16[128,2048]{1,0:T(8,128)(2,1)}, bf16[128,2048]{1,0:T(8,128)(2,1)}, u32[]{:S(2)}, u32[]{:S(2)}) collective-permute-start(bf16[128,2048]{1,0:T(8,128)(2,1)} %collective-permute-done.8.rest_4_), channel_id=1, source_target_pairs={{0,4},{1,5},{2,6},{3,7},{4,8},{5,9},{6,10},{7,11},{8,12},{9,13},{1... | collective-permute-start | bytes 1572872 | tf_op jit(solution)/shard_map/ppermute | solution.py:351
  148.9 12.1 %collective-permute-start.1 = (bf16[128,128]{1,0:T(8,128)(2,1)S(1)}, bf16[128,128]{1,0:T(8,128)(2,1)S(1)}, u32[]{:S(2)}, u32[]{:S(2)}) collective-permute-start(bf16[128,128]{1,0:T(8,128)(2,1)S(1)} %get-tuple-element.14), channel_id=1, source_target_pairs={{0,4},{1,5},{2,6},{3,7},{4,8},{5,9},{6,10},{7,11},{8,12},{9,13},{1... | collective-permute-start | bytes 98312 | tf_op jit(solution)/shard_map/ppermute | solution.py:369
  161.0 6.9 %collective-permute-start.2 = (bf16[128,128]{1,0:T(8,128)(2,1)S(1)}, bf16[128,128]{1,0:T(8,128)(2,1)S(1)}, u32[]{:S(2)}, u32[]{:S(2)}) collective-permute-start(bf16[128,128]{1,0:T(8,128)(2,1)S(1)} %collective-permute-done.1), channel_id=1, source_target_pairs={{0,4},{1,5},{2,6},{3,7},{4,8},{5,9},{6,10},{7,11},{8,12},{9,13},{1... | collective-permute-start | bytes 98312 | tf_op jit(solution)/shard_map/ppermute | solution.py:369
  163.2 39.3 %collective-permute-start.6 = (bf16[128,2048]{1,0:T(8,128)(2,1)}, bf16[128,2048]{1,0:T(8,128)(2,1)S(1)}, u32[]{:S(2)}, u32[]{:S(2)}) collective-permute-start(bf16[128,2048]{1,0:T(8,128)(2,1)} %get-tuple-element.8.rest_0_), channel_id=1, source_target_pairs={{0,2},{1,3},{2,0},{3,1},{4,6},{5,7},{6,4},{7,5},{8,10},{9,11},{10,... | collective-permute-start | bytes 1572872 | tf_op jit(solution)/shard_map/ppermute | solution.py:352
  164.5 38.1 %collective-permute-start.5 = (bf16[128,2048]{1,0:T(8,128)(2,1)}, bf16[128,2048]{1,0:T(8,128)(2,1)S(1)}, u32[]{:S(2)}, u32[]{:S(2)}) collective-permute-start(bf16[128,2048]{1,0:T(8,128)(2,1)} %get-tuple-element.8.rest_0_), channel_id=1, source_target_pairs={{0,1},{1,0},{2,3},{3,2},{4,5},{5,4},{6,7},{7,6},{8,9},{9,8},{10,11... | collective-permute-start | bytes 1572872 | tf_op jit(solution)/shard_map/ppermute | solution.py:353
  166.5 36.6 %collective-permute-start.10 = (bf16[128,2048]{1,0:T(8,128)(2,1)}, bf16[128,2048]{1,0:T(8,128)(2,1)S(1)}, u32[]{:S(2)}, u32[]{:S(2)}) collective-permute-start(bf16[128,2048]{1,0:T(8,128)(2,1)} %collective-permute-done.8.rest_4_), channel_id=1, source_target_pairs={{0,2},{1,3},{2,0},{3,1},{4,6},{5,7},{6,4},{7,5},{8,10},{9,11},{10,... | collective-permute-start | bytes 1572872 | tf_op jit(solution)/shard_map/ppermute | solution.py:352
  166.7 36.4 %collective-permute-start.14 = (bf16[128,2048]{1,0:T(8,128)(2,1)}, bf16[128,2048]{1,0:T(8,128)(2,1)S(1)}, u32[]{:S(2)}, u32[]{:S(2)}) collective-permute-start(bf16[128,2048]{1,0:T(8,128)(2,1)} %collective-permute-done.12.rest_8_), channel_id=1, source_target_pairs={{0,2},{1,3},{2,0},{3,1},{4,6},{5,7},{6,4},{7,5},{8,10},{9,11},{10,... | collective-permute-start | bytes 1572872 | tf_op jit(solution)/shard_map/ppermute | solution.py:352
  168.0 31.9 %collective-permute-start.3 = (bf16[3,128,128]{2,1,0:T(8,128)(2,1)S(1)}, bf16[3,128,128]{2,1,0:T(8,128)(2,1)S(1)}, u32[]{:S(2)}, u32[]{:S(2)}) collective-permute-start(bf16[3,128,128]{2,1,0:T(8,128)(2,1)S(1)} %get-tuple-element.12), channel_id=1, source_target_pairs={{0,2},{1,3},{2,0},{3,1},{4,6},{5,7},{6,4},{7,5},{8,10},{9,11},{10,... | collective-permute-start | bytes 294920 | tf_op jit(solution)/shard_map/ppermute | solution.py:371
  199.8 3.7 %collective-permute-start.4 = (bf16[6,128,128]{2,1,0:T(8,128)(2,1)S(1)}, bf16[6,128,128]{2,1,0:T(8,128)(2,1)S(1)}, u32[]{:S(2)}, u32[]{:S(2)}) collective-permute-start(bf16[6,128,128]{2,1,0:T(8,128)(2,1)S(1)} %pad_maximum_fusion.1), channel_id=1, source_target_pairs={{0,1},{1,0},{2,3},{3,2},{4,5},{5,4},{6,7},{7,6},{8,9},{9,8},{10,11... | collective-permute-start | bytes 589832 | tf_op jit(solution)/shard_map/ppermute | solution.py:372
  202.5 3.7 %copy-start.4 = (bf16[128,2048]{1,0:T(8,128)(2,1)}, bf16[128,2048]{1,0:T(8,128)(2,1)S(1)}, u32[]{:S(2)}) copy-start(bf16[128,2048]{1,0:T(8,128)(2,1)S(1)} %collective-permute-done.6.rest_2_) | copy-start | bytes 1572868
  202.5 3.7 %collective-permute-start.9 = (bf16[128,2048]{1,0:T(8,128)(2,1)}, bf16[128,2048]{1,0:T(8,128)(2,1)S(1)}, u32[]{:S(2)}, u32[]{:S(2)}) collective-permute-start(bf16[128,2048]{1,0:T(8,128)(2,1)} %collective-permute-done.8.rest_4_), channel_id=1, source_target_pairs={{0,1},{1,0},{2,3},{3,2},{4,5},{5,4},{6,7},{7,6},{8,9},{9,8},{10,11... | collective-permute-start | bytes 1572872 | tf_op jit(solution)/shard_map/ppermute | solution.py:353
  202.6 2.7 %copy-start.5 = (bf16[128,2048]{1,0:T(8,128)(2,1)}, bf16[128,2048]{1,0:T(8,128)(2,1)S(1)}, u32[]{:S(2)}) copy-start(bf16[128,2048]{1,0:T(8,128)(2,1)S(1)} %collective-permute-done.5.rest_1_) | copy-start | bytes 1572868
  202.6 3.6 %collective-permute-start.7 = (bf16[128,2048]{1,0:T(8,128)(2,1)S(1)}, bf16[128,2048]{1,0:T(8,128)(2,1)S(1)}, u32[]{:S(2)}, u32[]{:S(2)}) collective-permute-start(bf16[128,2048]{1,0:T(8,128)(2,1)S(1)} %collective-permute-done.6.rest_2_), channel_id=1, source_target_pairs={{0,1},{1,0},{2,3},{3,2},{4,5},{5,4},{6,7},{7,6},{8,9},{9,8},{10,11... | collective-permute-start | bytes 1572872 | tf_op jit(solution)/shard_map/ppermute | solution.py:354
  203.0 3.1 %copy-start.6 = (bf16[128,2048]{1,0:T(8,128)(2,1)}, bf16[128,2048]{1,0:T(8,128)(2,1)S(1)}, u32[]{:S(2)}) copy-start(bf16[128,2048]{1,0:T(8,128)(2,1)S(1)} %collective-permute-done.10.rest_6_) | copy-start | bytes 1572868
  203.0 3.2 %collective-permute-start.13 = (bf16[128,2048]{1,0:T(8,128)(2,1)}, bf16[128,2048]{1,0:T(8,128)(2,1)S(1)}, u32[]{:S(2)}, u32[]{:S(2)}) collective-permute-start(bf16[128,2048]{1,0:T(8,128)(2,1)} %collective-permute-done.12.rest_8_), channel_id=1, source_target_pairs={{0,1},{1,0},{2,3},{3,2},{4,5},{5,4},{6,7},{7,6},{8,9},{9,8},{10,11... | collective-permute-start | bytes 1572872 | tf_op jit(solution)/shard_map/ppermute | solution.py:353
  203.1 3.8 %copy-start.7 = (bf16[128,2048]{1,0:T(8,128)(2,1)}, bf16[128,2048]{1,0:T(8,128)(2,1)S(1)}, u32[]{:S(2)}) copy-start(bf16[128,2048]{1,0:T(8,128)(2,1)S(1)} %collective-permute-done.14.rest_10_) | copy-start | bytes 1572868
  203.1 3.7 %collective-permute-start.11 = (bf16[128,2048]{1,0:T(8,128)(2,1)S(1)}, bf16[128,2048]{1,0:T(8,128)(2,1)S(1)}, u32[]{:S(2)}, u32[]{:S(2)}) collective-permute-start(bf16[128,2048]{1,0:T(8,128)(2,1)S(1)} %collective-permute-done.10.rest_6_), channel_id=1, source_target_pairs={{0,1},{1,0},{2,3},{3,2},{4,5},{5,4},{6,7},{7,6},{8,9},{9,8},{10,11... | collective-permute-start | bytes 1572872 | tf_op jit(solution)/shard_map/ppermute | solution.py:354
  203.6 4.1 %collective-permute-start.15 = (bf16[128,2048]{1,0:T(8,128)(2,1)S(1)}, bf16[128,2048]{1,0:T(8,128)(2,1)S(1)}, u32[]{:S(2)}, u32[]{:S(2)}) collective-permute-start(bf16[128,2048]{1,0:T(8,128)(2,1)S(1)} %collective-permute-done.14.rest_10_), channel_id=1, source_target_pairs={{0,1},{1,0},{2,3},{3,2},{4,5},{5,4},{6,7},{7,6},{8,9},{9,8},{10,11... | collective-permute-start | bytes 1572872 | tf_op jit(solution)/shard_map/ppermute | solution.py:354
  206.1 1.5 copy-start.8
  206.2 1.5 copy-start.9
  206.2 1.4 copy-start.10
  206.9 0.8 copy-start.11
  207.6 0.8 copy-start.12
  217.5 1.4 copy-start.3
